TPU v7x, 32 devices: a whole 2x2x4 slice. The times are simulated.
32 devices in a mesh: blk: 8 (over y, x, core), feat: 4 (over z).
Axes of the slice: x: 2, y: 2, z: 4, core: 2. Of those that a mesh axis runs over, the one named last changes fastest.
Arguments:
- node_feats: bfloat16 [8192, 512], P('blk', 'feat'), may hold values from -6 to 6
- weight: bfloat16 [512, 512], P(None, 'feat'), may hold values from -0.25 to 0.25
- tile_value: bfloat16 [8, 5, 8, 128, 128], P('blk'), may hold values from -0.75 to 0.75
- tile_row: int32 [8, 5, 8], P('blk'), may hold values from 0 to 7
- tile_col: int32 [8, 5, 8], P('blk'), may hold values from 0 to 7
- tile_count: int32 [8, 5], P('blk'), may hold values from 2 to 8, as said below
- grad_out: bfloat16 [8192, 512], P('blk', 'feat'), may hold values from -6 to 6
Outputs:
- output_y: bfloat16 [8192, 512], P('blk', 'feat')
- grad_x: bfloat16 [8192, 512], P('blk', 'feat')
- grad_w: float32 [512, 512], P(None, 'feat')
Inputs may be any that keep to these rules, and one draw needn't show every extreme that they name: `tile_count`: in every draw one owner has all 8 slots live for every distance; owners differ in how many tiles they hold.
All inputs are finite; a program needn't handle non-finite values.
Results may differ from a plain program's by a relative error of at most 0.0062.
Values may be sent and summed in bfloat16 or wider, within the bound.
A program may use at most 64 MiB of HBM per device.

v0:
```python
import functools

import jax
import jax.numpy as jnp
from jax import lax
from jax.experimental import pallas as pl
from jax.experimental.pallas import tpu as pltpu
from jax.sharding import PartitionSpec as P

MESH = pl.DeviceIdType.MESH
BF = jnp.bfloat16
F32 = jnp.float32


def stage_factors(count, rows):
    factors = []
    while count > 1:
        size = max(f for f in range(2, 17) if count % f == 0 and rows % (16 * f) == 0)
        factors.append(size)
        count //= size
    return factors


def remote(src, dst, send, recv, where):
    return pltpu.make_async_remote_copy(
        src_ref=src, dst_ref=dst, send_sem=send, recv_sem=recv, device_id=where, device_id_type=MESH
    )


def layer_kernel(
    dims, x, w_in, tv_in, tr, tc, cnt, go_in, y, gx, gw,
    xg, wz, w, tv, go, tt, prod, gp, sent, got, gg, gwb, *rest
):
    nb, nz, offs, slots, blocks, side, width, ahead, factors = dims
    stages = len(factors)
    hid, rest = rest[:offs], rest[offs:]
    gathered, summed = rest[:stages], rest[stages : 2 * stages]
    (xs, xr, xl, ws, wr, hs, hr, gs, gr, zs, zr, zl, near) = rest[2 * stages : 2 * stages + 13]
    psems = rest[2 * stages + 13 :]
    reach = (offs - 1) // 2
    per_block = slots // blocks
    me = lax.axis_index("feat")
    own = lax.axis_index("blk")
    turn = 1 - 2 * lax.rem(own, 2)
    OWN, PAIR, CROSS, AHEAD, BEHIND = range(5)
    lean = (0, 1, -1, 2, -2)

    def offset_of(role):
        return reach + lean[role] * turn

    def owner_at(role):
        return {"blk": lax.rem(own + lean[role] * turn + nb, nb)}

    local = [
        pltpu.make_async_copy(w_in, w, near.at[0]),
        pltpu.make_async_copy(x, xg.at[:, pl.ds(pl.multiple_of(me * width, width), width)], near.at[1]),
        pltpu.make_async_copy(
            w_in.at[pl.ds(pl.multiple_of(me * width, width), width), :],
            wz.at[:, pl.ds(pl.multiple_of(me * w.shape[1], w.shape[1]), w.shape[1])],
            near.at[2],
        ),
        pltpu.make_async_copy(tv_in.at[0], tv, near.at[3]),
        pltpu.make_async_copy(go_in, go, near.at[4]),
    ]
    for copy in local:
        copy.start()

    def rows(b):
        return pl.ds(pl.multiple_of(b * side, side), side)

    def cols(z):
        return pl.ds(pl.multiple_of(z * width, width), width)

    def stage_peer(stage, step):
        stride = 1
        for f in factors[:stage]:
            stride *= f
        size = factors[stage]
        digit = lax.rem(own // stride, size)
        other = lax.rem(digit + step, size)
        return digit, other, own + (other - digit) * stride

    barrier = pltpu.get_barrier_semaphore()
    greeted = 0
    for step in range(1, nz):
        pl.semaphore_signal(barrier, inc=1, device_id={"feat": lax.rem(me + step, nz)}, device_id_type=MESH)
        greeted += 1
    for role in (PAIR, AHEAD, BEHIND) if stages > 1 else ():
        pl.semaphore_signal(barrier, inc=1, device_id=owner_at(role), device_id_type=MESH)
        greeted += 1
    for stage in range(stages):
        for step in range(1, factors[stage]):
            _, _, peer = stage_peer(stage, step)
            pl.semaphore_signal(barrier, inc=1, device_id={"blk": peer}, device_id_type=MESH)
            greeted += 1
    pl.semaphore_wait(barrier, greeted)

    def line_send(src_of, dst, send, recv, b):
        for d in (1, 2):
            for sign in (-1, 1):
                t = me + sign * d

                @pl.when((t >= 0) & (t < nz))
                def _():
                    remote(
                        src_of(b), dst.at[rows(b), cols(me)], send.at[t, b], recv.at[me, b], {"feat": t}
                    ).start()

    def line_recv(dst, relay, recv, b):
        for d in range(1, nz):
            for sign in (-1, 1):
                s = me + sign * d

                @pl.when((s >= 0) & (s < nz))
                def _():
                    piece = dst.at[rows(b), cols(s)]
                    remote(piece, piece, relay.at[s, b], recv.at[s, b], {"feat": s}).wait_recv()
                    if d >= 2:
                        t = me - sign

                        @pl.when((t >= 0) & (t < nz))
                        def _():
                            remote(piece, piece, relay.at[s, b], recv.at[s, b], {"feat": t}).start()

    def line_drain(dst, send, relay, recv, b):
        for d in (1, 2):
            for sign in (-1, 1):
                t = me + sign * d

                @pl.when((t >= 0) & (t < nz))
                def _():
                    piece = dst.at[rows(b), cols(me)]
                    remote(piece, piece, send.at[t, b], recv.at[me, b], {"feat": t}).wait_send()

        for d in range(2, nz):
            for sign in (-1, 1):
                s = me + sign * d
                t = me - sign

                @pl.when((s >= 0) & (s < nz) & (t >= 0) & (t < nz))
                def _():
                    piece = dst.at[rows(b), cols(s)]
                    remote(piece, piece, relay.at[s, b], recv.at[s, b], {"feat": t}).wait_send()

    def x_piece(b):
        return x.at[rows(b), :]

    for b in range(min(ahead, blocks)):
        line_send(x_piece, xg, xs, xr, b)
    for step in range(1, nz):
        d = lax.rem(me + step, nz)
        remote(w_in.at[cols(d), :], wz.at[:, cols(me)], ws.at[step], wr.at[nz - step], {"feat": d}).start()
    for copy in local[:4]:
        copy.wait()

    landing = {PAIR: PAIR, AHEAD: BEHIND, BEHIND: AHEAD}

    def hid_copy(role, b):
        return remote(hid[OWN].at[b], hid[landing[role]].at[b], hs.at[role, b], hr.at[landing[role], b], owner_at(role))

    def hid_wait(role, b):
        remote(hid[role].at[b], hid[role].at[b], hs.at[role, b], hr.at[role, b], owner_at(PAIR)).wait_recv()

    def hid_passed(b):
        return remote(hid[AHEAD].at[b], hid[CROSS].at[b], hs.at[CROSS, b], hr.at[CROSS, b], owner_at(PAIR))

    def hid_relay(b):
        hid_wait(AHEAD, b)
        hid_passed(b).start()

    def forward_step(b, carry):
        @pl.when(b + ahead < blocks)
        def _():
            line_send(x_piece, xg, xs, xr, b + ahead)

        for role in range(offs):
            for s in range(per_block):
                slot = b * per_block + s
                tt[role, slot] = tv[offset_of(role), slot].T
        line_recv(xg, xl, xr, b)
        hid[OWN][b] = jnp.dot(xg[rows(b), :], w[...], preferred_element_type=F32).astype(BF)
        hid_copy(PAIR, b).start()
        hid_copy(AHEAD, b).start()
        hid_copy(BEHIND, b).start()

        @pl.when(b >= 1)
        def _():
            hid_relay(b - 1)

        return carry

    lax.fori_loop(0, blocks, forward_step, 0)

    hid_relay(blocks - 1)

    def forward_products(role):
        k = offset_of(role)
        for s in range(slots):
            prod[role, s] = jnp.dot(tv[k, s], hid[role][tc[k, 0, s]], preferred_element_type=F32)

    forward_products(OWN)
    forward_products(AHEAD)
    for role in (PAIR, BEHIND, CROSS):
        for b in range(blocks):
            hid_wait(role, b)
        forward_products(role)
    local[4].wait()

    def weight_of(table, k, s, b):
        return jnp.where((table[k, 0, s] == b) & (s < cnt[0, k]), 1.0, 0.0).astype(F32)

    def pointwise(b, carry):
        v = hid[OWN][b].astype(F32)
        for role in range(offs):
            for s in range(slots):
                v = v + prod[role, s] * weight_of(tr, offset_of(role), s, b)
        sigma = jax.nn.sigmoid(v)
        y[rows(b), :] = (v * sigma).astype(BF)
        slope = sigma * (1.0 + v * (1.0 - sigma))
        gp[b] = (go[rows(b), :].astype(F32) * slope).astype(BF)
        return carry

    lax.fori_loop(0, blocks, pointwise, 0)

    for role in range(offs):
        for s in range(slots):
            prod[role, s] = jnp.dot(tt[role, s], gp[tr[offset_of(role), 0, s]], preferred_element_type=F32)

    def column_sum(role, c, start):
        total = start
        for s in range(slots):
            term = prod[role, s] * weight_of(tc, offset_of(role), s, c)
            total = term if total is None else total + term
        return total

    target = {PAIR: PAIR, CROSS: PAIR, AHEAD: AHEAD, BEHIND: BEHIND}
    arrives = {PAIR: PAIR, CROSS: CROSS, AHEAD: BEHIND, BEHIND: AHEAD}

    def sum_copy(role, c):
        return remote(
            sent.at[role, c], got.at[arrives[role], c], gs.at[role, c], gr.at[arrives[role], c], owner_at(target[role])
        )

    def sum_wait(role, c):
        remote(got.at[role, c], got.at[role, c], gs.at[role, c], gr.at[role, c], owner_at(PAIR)).wait_recv()

    def send_sum(role, c):
        sent[role, c] = column_sum(role, c, None).astype(BF)
        sum_copy(role, c).start()

    def send_joint(c):
        sum_wait(CROSS, c)
        sent[AHEAD, c] = column_sum(AHEAD, c, got[CROSS, c].astype(F32)).astype(BF)
        sum_copy(AHEAD, c).start()

    gw[...] = jnp.zeros_like(gw)

    def gg_piece(b):
        return gg.at[rows(b), cols(me)]

    def make_grad(b):
        total = column_sum(OWN, b, gp[b].astype(F32))
        for role in (PAIR, BEHIND, AHEAD):
            sum_wait(role, b)
            total = total + got[role, b].astype(F32)
        grad = total.astype(BF)
        gg[rows(b), cols(me)] = grad
        line_send(gg_piece, gg, zs, zr, b)
        gw[...] += lax.dot_general(
            xg[rows(b), :], grad, (((0,), (0,)), ((), ())), preferred_element_type=F32
        )

    def finish(b):
        line_recv(gg, zl, zr, b)
        gx[rows(b), :] = lax.dot_general(
            gg[rows(b), :], wz[...], (((1,), (1,)), ((), ())), preferred_element_type=F32
        ).astype(BF)

    for step in range(1, nz):
        d = lax.rem(me + step, nz)
        piece = wz.at[:, cols(d)]
        remote(w_in.at[cols(d), :], piece, ws.at[step], wr.at[step], {"feat": d}).wait_recv()

    lag, tail = 2, 4

    def backward_step(c, carry):
        @pl.when(c < blocks)
        def _():
            send_sum(CROSS, c)
            send_sum(BEHIND, c)
            send_sum(PAIR, c)

        @pl.when((c >= 1) & (c <= blocks))
        def _():
            send_joint(c - 1)

        @pl.when(c >= lag)
        def _():
            make_grad(c - lag)

        @pl.when(c >= tail)
        def _():
            finish(c - tail)

        return carry

    lax.fori_loop(0, blocks + lag, backward_step, 0)

    gwb[...] = gw[...].astype(BF)
    height = gw.shape[0]
    for stage in range(stages):
        size = factors[stage]
        chunk = height // size
        src, buf, out = gwb if stage == 0 else summed[stage - 1], gathered[stage], summed[stage]
        rs_s, rs_r, ag_s, ag_r = psems[4 * stage : 4 * stage + 4]

        def part(q):
            return pl.ds(pl.multiple_of(q * chunk, chunk), chunk)

        for step in range(1, size):
            _, other, peer = stage_peer(stage, step)
            remote(src.at[part(other), :], buf.at[step], rs_s.at[step], rs_r.at[step], {"blk": peer}).start()
        if stage == 0:
            for b in range(blocks + lag - tail, blocks):
                finish(b)
        digit, _, _ = stage_peer(stage, 1)
        if stage == 0:
            total = gw[part(digit), :]
        else:
            total = src[part(digit), :].astype(F32)
        for step in range(1, size):
            _, _, peer = stage_peer(stage, step)
            remote(buf.at[step], buf.at[step], rs_s.at[step], rs_r.at[step], {"blk": peer}).wait_recv()
            total = total + buf[step].astype(F32)
        out[part(digit), :] = total.astype(BF)
        for step in range(1, size):
            _, _, peer = stage_peer(stage, step)
            piece = out.at[part(digit), :]
            remote(piece, piece, ag_s.at[step], ag_r.at[step], {"blk": peer}).start()
        for step in range(1, size):
            _, other, peer = stage_peer(stage, size - step)
            piece = out.at[part(other), :]
            remote(piece, piece, ag_s.at[step], ag_r.at[step], {"blk": peer}).wait_recv()
    gw[...] = (summed[-1] if stages else gwb)[...].astype(F32)

    for stage in range(stages):
        size = factors[stage]
        chunk = height // size
        src, buf, out = gwb if stage == 0 else summed[stage - 1], gathered[stage], summed[stage]
        rs_s, rs_r, ag_s, ag_r = psems[4 * stage : 4 * stage + 4]
        for step in range(1, size):
            _, other, peer = stage_peer(stage, step)
            remote(buf.at[step], buf.at[step], rs_s.at[step], rs_r.at[step], {"blk": peer}).wait_send()
            remote(buf.at[step], buf.at[step], ag_s.at[step], ag_r.at[step], {"blk": peer}).wait_send()
    for step in range(1, nz):
        d = lax.rem(me + step, nz)
        remote(w_in.at[cols(d), :], wz.at[:, cols(me)], ws.at[step], wr.at[step], {"feat": d}).wait_send()

    def drain(b, carry):
        line_drain(xg, xs, xl, xr, b)
        line_drain(gg, zs, zl, zr, b)
        for role in (PAIR, AHEAD, BEHIND):
            hid_copy(role, b).wait_send()
        hid_passed(b).wait_send()
        for role in (PAIR, CROSS, AHEAD, BEHIND):
            sum_copy(role, b).wait_send()
        return carry

    lax.fori_loop(0, blocks, drain, 0)


def on_device(nb, nz, x, w, tv, tr, tc, cnt, go):
    offs, slots, side = tv.shape[1], tv.shape[2], tv.shape[-1]
    height, width = x.shape
    blocks = height // side
    depth, out_width = w.shape
    factors = stage_factors(nb, depth)
    dims = (nb, nz, offs, slots, blocks, side, width, 3, tuple(factors))
    vmem = pl.BlockSpec(memory_space=pltpu.VMEM)
    hbm = pl.BlockSpec(memory_space=pltpu.HBM)
    smem = pl.BlockSpec(memory_space=pltpu.SMEM)
    dma = pltpu.SemaphoreType.DMA
    psems = []
    for f in factors:
        psems += [dma((f,))] * 4
    line = [dma((nz, blocks))] * 3
    banded = [dma((offs, blocks))] * 2
    return pl.pallas_call(
        functools.partial(layer_kernel, dims),
        out_shape=(
            jax.ShapeDtypeStruct((height, out_width), BF),
            jax.ShapeDtypeStruct((height, width), BF),
            jax.ShapeDtypeStruct((depth, out_width), F32),
        ),
        in_specs=[hbm, hbm, hbm, smem, smem, smem, hbm],
        out_specs=(vmem, vmem, vmem),
        scratch_shapes=[
            pltpu.VMEM((height, nz * width), BF),
            pltpu.VMEM((width, nz * out_width), BF),
            pltpu.VMEM((depth, out_width), BF),
            pltpu.VMEM((offs, slots, side, side), BF),
            pltpu.VMEM((height, out_width), BF),
            pltpu.VMEM((offs, slots, side, side), BF),
            pltpu.VMEM((offs, slots, side, out_width), F32),
            pltpu.VMEM((blocks, side, out_width), BF),
            pltpu.VMEM((offs, blocks, side, out_width), BF),
            pltpu.VMEM((offs, blocks, side, out_width), BF),
            pltpu.VMEM((height, nz * out_width), BF),
            pltpu.VMEM((depth, out_width), BF),
        ]
        + [pltpu.VMEM((blocks, side, out_width), BF)] * offs
        + [pltpu.VMEM((f, depth // f, out_width), BF) for f in factors]
        + [pltpu.VMEM((depth, out_width), BF) for f in factors]
        + line
        + [dma((nz,)), dma((nz,))]
        + banded
        + banded
        + line
        + [dma((5,))]
        + psems,
        compiler_params=pltpu.CompilerParams(
            collective_id=0, has_side_effects=True, vmem_limit_bytes=63 * 1024 * 1024
        ),
    )(x, w, tv, jnp.swapaxes(tr, 0, 1), jnp.swapaxes(tc, 0, 1), cnt, go)


def solution(mesh):
    return jax.shard_map(
        functools.partial(on_device, mesh.shape["blk"], mesh.shape["feat"]),
        mesh=mesh,
        in_specs=(
            P("blk", "feat"),
            P(None, "feat"),
            P("blk", None, None, None, None),
            P("blk", None, None),
            P("blk", None, None),
            P("blk", None),
            P("blk", "feat"),
        ),
        out_specs=(P("blk", "feat"), P("blk", "feat"), P(None, "feat")),
        check_vma=False,
    )
```

profile of v0, /device:TPU:0, one launch (start us, length us, event | category | flops | bytes accessed | tf_op | source)
XLA Modules:
  0.0 83.4 jit_solution(17719091344102027336)
XLA Ops:
  0.6 77.8 %shard_map.94 = (bf16[1024,128]{1,0:T(8,128)(2,1)}, bf16[1024,128]{1,0:T(8,128)(2,1)}, f32[512,128]{1,0:T(8,128)}) custom-call(bf16[1024,128]{1,0:T(8,128)(2,1)} %x.1, bf16[512,128]{1,0:T(8,128)(2,1)} %w_in.1, bf16[1,5,8,128,128]{4,3,2,1,0:T(8,128)(2,1)} %tv_in.1, s32[5,1,8]{2,1,0:T(1,128)} %bitcast.2, s32[5,1,8]{2,1,0:T(1,128)} %bitcast.3, s32[1,5]{1,0:T(1,128)} %cnt.1, ...), custom_call_target="tpu_custom_call" | custom-call | tf_op jit(solution)/shard_map/pallas_call | solution.py:388
  78.4 1.7 %copy.13 = bf16[1024,128]{1,0:T(8,128)(2,1)} copy(bf16[1024,128]{1,0:T(8,128)(2,1)} %get-tuple-element.6) | data formatting | bytes 524288
  80.1 1.7 %copy.14 = bf16[1024,128]{1,0:T(8,128)(2,1)} copy(bf16[1024,128]{1,0:T(8,128)(2,1)} %get-tuple-element.7) | data formatting | bytes 524288
  81.8 1.7 %copy.15 = f32[512,128]{1,0:T(8,128)} copy(f32[512,128]{1,0:T(8,128)} %get-tuple-element.8) | data formatting | bytes 524288
where the time goes:
time: 83.7 us; the launch traced here: 83.4 us
  Pallas kernels  77.8 us (93%)
  local copies, waits for them, and re-layouts  5.01 us (6%)
    pallas_call x1, Pallas kernels, on_device(): pl.pallas_call(functools.partial(layer_kernel, dims), out_shape=(jax.Shap...  77.8 us
    unnamed x3, local copies, waits for them, and re-layouts  5.01 us

commit v1 on v0

v1 whole, which is shorter than its diff:
```python
import functools

import jax
import jax.numpy as jnp
from jax import lax
from jax.experimental import pallas as pl
from jax.experimental.pallas import tpu as pltpu
from jax.sharding import PartitionSpec as P

MESH = pl.DeviceIdType.MESH
BF = jnp.bfloat16
F32 = jnp.float32


def stage_factors(count, rows):
    factors = []
    while count > 1:
        size = max(f for f in range(2, 17) if count % f == 0 and rows % (16 * f) == 0)
        factors.append(size)
        count //= size
    return factors


def remote(src, dst, send, recv, where):
    return pltpu.make_async_remote_copy(
        src_ref=src, dst_ref=dst, send_sem=send, recv_sem=recv, device_id=where, device_id_type=MESH
    )


def layer_kernel(
    dims, x, w_in, tv_in, tr, tc, cnt, go_in, y, gx, gw,
    xg, wg, tv, go, tt, prod, acc, gp, sent, got, gg, gwb, pe, ge, *rest
):
    nb, nz, offs, slots, blocks, side, width, ow, factors = dims
    stages = len(factors)
    hid, rest = rest[:offs], rest[offs:]
    gathered, summed = rest[:stages], rest[stages : 2 * stages]
    (xs, xr, xl, xb, hs, hr, gs, gr, zs, zr, es, ges, ger, ws, wr, ks, kr, near) = rest[2 * stages : 2 * stages + 18]
    psems = rest[2 * stages + 18 :]
    reach = (offs - 1) // 2
    half = nz // 2
    me = lax.axis_index("feat")
    own = lax.axis_index("blk")
    core = lax.rem(own, 2)
    turn = 1 - 2 * core
    OWN, PAIR, CROSS, AHEAD, BEHIND = range(5)
    lean = (0, 1, -1, 2, -2)
    lower = me < half
    inner = jnp.where(lower, half - 1, half)
    other = nz - 1 - inner
    is_inner = me == inner
    ends = range(1, half)
    relayed = (blocks // 2 - 1, blocks // 2)

    def end_at(j):
        return jnp.where(lower, half - 1 - j, half + j)

    def in_relay(b):
        return (b >= relayed[0]) & (b <= relayed[1])

    def offset_of(role):
        return reach + lean[role] * turn

    def owner_at(role):
        return {"blk": lax.rem(own + lean[role] * turn + nb, nb)}

    def rows(b):
        return pl.ds(pl.multiple_of(b * side, side), side)

    def xcols(z):
        return pl.ds(pl.multiple_of(z * width, width), width)

    def ocols(z):
        return pl.ds(pl.multiple_of(z * ow, ow), ow)

    local = [
        pltpu.make_async_copy(w_in, wg.at[:, ocols(me)], near.at[0]),
        pltpu.make_async_copy(x, xg.at[:, xcols(me)], near.at[1]),
        pltpu.make_async_copy(tv_in.at[0], tv, near.at[2]),
        pltpu.make_async_copy(go_in, go, near.at[3]),
    ]
    for copy in local:
        copy.start()

    def stage_peer(stage, step):
        stride = 1
        for f in factors[:stage]:
            stride *= f
        size = factors[stage]
        digit = lax.rem(own // stride, size)
        there = lax.rem(digit + step, size)
        return digit, there, own + (there - digit) * stride

    barrier = pltpu.get_barrier_semaphore()
    greeted = 0
    for step in range(1, nz):
        pl.semaphore_signal(barrier, inc=1, device_id={"feat": lax.rem(me + step, nz)}, device_id_type=MESH)
        greeted += 1
    for role in (PAIR, AHEAD, BEHIND) if stages > 1 else ():
        pl.semaphore_signal(barrier, inc=1, device_id=owner_at(role), device_id_type=MESH)
        greeted += 1
    for stage in range(stages):
        for step in range(1, factors[stage]):
            _, _, peer = stage_peer(stage, step)
            pl.semaphore_signal(barrier, inc=1, device_id={"blk": peer}, device_id_type=MESH)
            greeted += 1
    pl.semaphore_wait(barrier, greeted)

    depth = w_in.shape[0]

    def part_of(piece):
        return pl.ds(pl.multiple_of(piece * (depth // 2), depth // 2), depth // 2)

    def x_copy(way, b):
        return remote(
            x.at[rows(b), :], xg.at[rows(b), xcols(me)], xs.at[way, b], xr.at[me, b], {"feat": (inner, other)[way]}
        )

    def x_relay(e, b):
        piece = xg.at[rows(b), xcols(e)]
        return remote(piece, piece, xl.at[e, b], xr.at[e, b], {"feat": other})

    def x_back(s, e, j, b):
        piece = xg.at[rows(b), xcols(s)]
        return remote(piece, piece, xb.at[j - 1, s, b], xr.at[s, b], {"feat": e})

    def x_wait(s, b):
        piece = xg.at[rows(b), xcols(s)]
        remote(piece, piece, xl.at[s, b], xr.at[s, b], {"feat": other}).wait_recv()

    def w_up():
        return remote(w_in.at[part_of(core), :], wg.at[part_of(core), ocols(me)], ws.at[0, 0], wr.at[me, core], {"feat": inner})

    def w_across(e):
        piece = wg.at[part_of(core), ocols(e)]
        return remote(piece, piece, ws.at[1, e], wr.at[e, core], owner_at(PAIR))

    def w_wait(e, piece):
        ref = wg.at[part_of(piece), ocols(e)]
        remote(ref, ref, ws.at[1, e], wr.at[e, piece], owner_at(PAIR)).wait_recv()

    def w_swap(sending):
        there = jnp.where(lower, half, 0)
        here = half - there
        r, c = (there, here) if sending else (here, there)
        piece = wg.at[
            pl.ds(pl.multiple_of(r * width, width), half * width), pl.ds(pl.multiple_of(c * ow, ow), half * ow)
        ]
        return remote(piece, piece, ks.at[0], kr.at[0], {"feat": other})

    @pl.when(is_inner)
    def _():
        for b in range(min(4, blocks)):
            x_copy(1, b).start()

    @pl.when(jnp.logical_not(is_inner))
    def _():
        for b in range(blocks):
            if b not in relayed:
                x_copy(1, b).start()
            x_copy(0, b).start()
            if b == 0:
                w_up().start()

    for copy in local[:3]:
        copy.wait()

    landing = {PAIR: PAIR, AHEAD: BEHIND, BEHIND: AHEAD}

    def hid_copy(role, b):
        return remote(hid[OWN].at[b], hid[landing[role]].at[b], hs.at[role, b], hr.at[landing[role], b], owner_at(role))

    def hid_wait(role, b):
        remote(hid[role].at[b], hid[role].at[b], hs.at[role, b], hr.at[role, b], owner_at(PAIR)).wait_recv()

    def hid_passed(b):
        return remote(hid[AHEAD].at[b], hid[CROSS].at[b], hs.at[CROSS, b], hr.at[CROSS, b], owner_at(PAIR))

    def hid_relay(b):
        hid_wait(AHEAD, b)
        hid_passed(b).start()

    def hid_down(j, b):
        return remote(pe.at[j - 1, b], hid[OWN].at[b], es.at[j - 1, b], hr.at[OWN, b], {"feat": end_at(j)})

    def spread(b):
        hid_copy(AHEAD, b).start()
        hid_copy(BEHIND, b).start()
        hid_copy(PAIR, b).start()

    lag = 2

    def forward_step(b, carry):
        @pl.when(is_inner)
        def _():
            @pl.when(b + 4 < blocks)
            def _():
                x_copy(1, b + 4).start()

            @pl.when(in_relay(b + 2))
            def _():
                for j in ends:
                    x_wait(end_at(j), b + 2)
                    x_relay(end_at(j), b + 2).start()

        per_block = slots // blocks
        for role in range(offs):
            for s in range(per_block):
                slot = b * per_block + s
                tt[role, slot] = tv[offset_of(role), slot].T

        @pl.when(is_inner)
        def _():
            for j in ends:
                @pl.when(jnp.logical_not(in_relay(b)))
                def _():
                    x_wait(end_at(j), b)
            for j in range(half):
                x_wait(nz - 1 - end_at(j), b)
            hid[OWN][b] = jnp.dot(xg[rows(b), :], wg[:, ocols(me)], preferred_element_type=F32).astype(BF)
            spread(b)

            @pl.when(b == 0)
            def _():
                for j in ends:
                    w_wait(end_at(j), core)
                    w_across(end_at(j)).start()
                for j in ends:
                    w_wait(end_at(j), 1 - core)

            for j in ends:
                pe[j - 1, b] = jnp.dot(xg[rows(b), :], wg[:, ocols(end_at(j))], preferred_element_type=F32).astype(BF)
                hid_down(j, b).start()
                x_back(me, end_at(j), j, b).start()

        @pl.when(jnp.logical_not(is_inner))
        def _():
            hid_wait(OWN, b)
            spread(b)

        @pl.when(b >= lag)
        def _():
            hid_relay(b - lag)

        return carry

    lax.fori_loop(0, blocks, forward_step, 0)

    def forward_products(role):
        k = offset_of(role)
        for s in range(slots):
            prod[role, s] = jnp.dot(tv[k, s], hid[role][tc[k, 0, s]], preferred_element_type=F32)

    def weight_of(table, k, s, b):
        return jnp.where((table[k, 0, s] == b) & (s < cnt[0, k]), 1.0, 0.0).astype(F32)

    def row_sum(role, b, total):
        for s in range(slots):
            total = total + prod[role, s] * weight_of(tr, offset_of(role), s, b)
        return total

    def gather_role(role):
        forward_products(role)

        def add(b, carry):
            start = hid[OWN][b].astype(F32) if role == OWN else acc[b]
            acc[b] = row_sum(role, b, start)
            return carry

        lax.fori_loop(0, blocks, add, 0)

    gather_role(OWN)
    for b in range(blocks):
        hid_wait(PAIR, b)
    gather_role(PAIR)
    for b in range(max(blocks - lag, 0), blocks):
        hid_relay(b)

    @pl.when(is_inner)
    def _():
        w_swap(True).start()
        for j in ends:
            for b in range(blocks):
                for step in range(1, nz):
                    s = lax.rem(me + step, nz)

                    @pl.when(s != end_at(j))
                    def _():
                        x_back(s, end_at(j), j, b).start()

    gather_role(AHEAD)
    for b in range(blocks):
        hid_wait(BEHIND, b)
    gather_role(BEHIND)
    local[3].wait()
    for b in range(blocks):
        hid_wait(CROSS, b)
    forward_products(CROSS)

    def pointwise(b, carry):
        v = row_sum(CROSS, b, acc[b])
        sigma = jax.nn.sigmoid(v)
        y[rows(b), :] = (v * sigma).astype(BF)
        slope = sigma * (1.0 + v * (1.0 - sigma))
        gp[b] = (go[rows(b), :].astype(F32) * slope).astype(BF)
        return carry

    lax.fori_loop(0, blocks, pointwise, 0)

    def backward_products(role):
        for s in range(slots):
            prod[role, s] = jnp.dot(tt[role, s], gp[tr[offset_of(role), 0, s]], preferred_element_type=F32)

    def column_sum(role, c, start):
        total = start
        for s in range(slots):
            term = prod[role, s] * weight_of(tc, offset_of(role), s, c)
            total = term if total is None else total + term
        return total

    target = {PAIR: PAIR, CROSS: PAIR, AHEAD: AHEAD, BEHIND: BEHIND}
    arrives = {PAIR: PAIR, CROSS: CROSS, AHEAD: BEHIND, BEHIND: AHEAD}

    def sum_copy(role, c):
        return remote(
            sent.at[role, c], got.at[arrives[role], c], gs.at[role, c], gr.at[arrives[role], c], owner_at(target[role])
        )

    def sum_wait(role, c):
        remote(got.at[role, c], got.at[role, c], gs.at[role, c], gr.at[role, c], owner_at(PAIR)).wait_recv()

    def send_sum(role, c):
        sent[role, c] = column_sum(role, c, None).astype(BF)
        sum_copy(role, c).start()

    def send_joint(c):
        sum_wait(CROSS, c)
        sent[AHEAD, c] = column_sum(AHEAD, c, got[CROSS, c].astype(F32)).astype(BF)
        sum_copy(AHEAD, c).start()

    def loop(step):
        def body(c, carry):
            step(c)
            return carry

        lax.fori_loop(0, blocks, body, 0)

    backward_products(CROSS)
    loop(lambda c: send_sum(CROSS, c))
    backward_products(BEHIND)
    backward_products(AHEAD)

    def send_far(c):
        send_sum(BEHIND, c)
        send_joint(c)

    loop(send_far)
    backward_products(PAIR)
    loop(lambda c: send_sum(PAIR, c))
    backward_products(OWN)

    gw[...] = jnp.zeros_like(gw)

    def g_copy(way, b):
        piece = gg.at[rows(b), ocols(me)]
        return remote(piece, piece, zs.at[way, b], zr.at[me, b], {"feat": (inner, other)[way]})

    def g_wait(s, b):
        piece = gg.at[rows(b), ocols(s)]
        remote(piece, piece, zs.at[0, b], zr.at[s, b], {"feat": other}).wait_recv()

    def make_grad(b):
        total = column_sum(OWN, b, gp[b].astype(F32))
        for role in (PAIR, BEHIND, AHEAD):
            sum_wait(role, b)
            total = total + got[role, b].astype(F32)
        grad = total.astype(BF)
        gg[rows(b), ocols(me)] = grad
        g_copy(1, b).start()

        @pl.when(jnp.logical_not(is_inner))
        def _():
            g_copy(0, b).start()
            for step in range(1, nz):
                x_wait(lax.rem(me + step, nz), b)

        gw[...] += lax.dot_general(xg[rows(b), :], grad, (((0,), (0,)), ((), ())), preferred_element_type=F32)

    def gx_down(j, b):
        return remote(ge.at[j - 1, b], gx.at[rows(b), :], ges.at[j - 1, b], ger.at[b], {"feat": end_at(j)})

    def finish(b):
        @pl.when(is_inner)
        def _():
            @pl.when(b == 0)
            def _():
                w_swap(False).wait_recv()

            for step in range(1, nz):
                g_wait(lax.rem(me + step, nz), b)

            def grad_of(z):
                return lax.dot_general(
                    gg[rows(b), :], wg[xcols(z), :], (((1,), (1,)), ((), ())), preferred_element_type=F32
                ).astype(BF)

            for j in ends:
                ge[j - 1, b] = grad_of(end_at(j))
                gx_down(j, b).start()
            gx[rows(b), :] = grad_of(me)

    behind = 3

    def backward_step(c, carry):
        make_grad(c)

        @pl.when(c >= behind)
        def _():
            finish(c - behind)

        return carry

    lax.fori_loop(0, blocks, backward_step, 0)

    gwb[...] = gw[...].astype(BF)
    height = gw.shape[0]
    for stage in range(stages):
        size = factors[stage]
        chunk = height // size
        src, buf, out = gwb if stage == 0 else summed[stage - 1], gathered[stage], summed[stage]
        rs_s, rs_r, ag_s, ag_r = psems[4 * stage : 4 * stage + 4]

        def part(q):
            return pl.ds(pl.multiple_of(q * chunk, chunk), chunk)

        for step in range(1, size):
            _, there, peer = stage_peer(stage, step)
            remote(src.at[part(there), :], buf.at[step], rs_s.at[step], rs_r.at[step], {"blk": peer}).start()
        if stage == 0:
            for b in range(blocks - behind, blocks - 1):
                finish(b)
        digit, _, _ = stage_peer(stage, 1)
        if stage == 0:
            total = gw[part(digit), :]
        else:
            total = src[part(digit), :].astype(F32)
        for step in range(1, size):
            _, _, peer = stage_peer(stage, step)
            remote(buf.at[step], buf.at[step], rs_s.at[step], rs_r.at[step], {"blk": peer}).wait_recv()
            total = total + buf[step].astype(F32)
        out[part(digit), :] = total.astype(BF)
        for step in range(1, size):
            _, _, peer = stage_peer(stage, step)
            piece = out.at[part(digit), :]
            remote(piece, piece, ag_s.at[step], ag_r.at[step], {"blk": peer}).start()
        if stage == 0:
            finish(blocks - 1)
        for step in range(1, size):
            _, there, peer = stage_peer(stage, size - step)
            piece = out.at[part(there), :]
            remote(piece, piece, ag_s.at[step], ag_r.at[step], {"blk": peer}).wait_recv()
    gw[...] = (summed[-1] if stages else gwb)[...].astype(F32)

    for stage in range(stages):
        size = factors[stage]
        buf = gathered[stage]
        rs_s, rs_r, ag_s, ag_r = psems[4 * stage : 4 * stage + 4]
        for step in range(1, size):
            _, _, peer = stage_peer(stage, step)
            remote(buf.at[step], buf.at[step], rs_s.at[step], rs_r.at[step], {"blk": peer}).wait_send()
            remote(buf.at[step], buf.at[step], ag_s.at[step], ag_r.at[step], {"blk": peer}).wait_send()

    def drain(b, carry):
        g_copy(1, b).wait_send()

        @pl.when(is_inner)
        def _():
            x_copy(1, b).wait_send()
            for j in ends:
                @pl.when(in_relay(b))
                def _():
                    x_relay(end_at(j), b).wait_send()

                hid_down(j, b).wait_send()
                gx_down(j, b).wait_send()
                for step in range(nz):
                    s = lax.rem(me + step, nz)

                    @pl.when(s != end_at(j))
                    def _():
                        x_back(s, end_at(j), j, b).wait_send()

        @pl.when(jnp.logical_not(is_inner))
        def _():
            @pl.when(jnp.logical_not(in_relay(b)))
            def _():
                x_copy(1, b).wait_send()

            x_copy(0, b).wait_send()
            g_copy(0, b).wait_send()
            remote(gx.at[rows(b), :], gx.at[rows(b), :], ges.at[0, b], ger.at[b], {"feat": inner}).wait_recv()

        for role in (PAIR, AHEAD, BEHIND):
            hid_copy(role, b).wait_send()
        hid_passed(b).wait_send()
        for role in (PAIR, CROSS, AHEAD, BEHIND):
            sum_copy(role, b).wait_send()
        return carry

    lax.fori_loop(0, blocks, drain, 0)

    @pl.when(is_inner)
    def _():
        w_swap(True).wait_send()
        for j in ends:
            w_across(end_at(j)).wait_send()

    @pl.when(jnp.logical_not(is_inner))
    def _():
        w_up().wait_send()


def on_device(nb, nz, x, w, tv, tr, tc, cnt, go):
    offs, slots, side = tv.shape[1], tv.shape[2], tv.shape[-1]
    height, width = x.shape
    blocks = height // side
    depth, ow = w.shape
    factors = stage_factors(nb, depth)
    dims = (nb, nz, offs, slots, blocks, side, width, ow, tuple(factors))
    spare = max(nz // 2 - 1, 1)
    vmem = pl.BlockSpec(memory_space=pltpu.VMEM)
    hbm = pl.BlockSpec(memory_space=pltpu.HBM)
    smem = pl.BlockSpec(memory_space=pltpu.SMEM)
    dma = pltpu.SemaphoreType.DMA
    psems = []
    for f in factors:
        psems += [dma((f,))] * 4
    banded = [dma((offs, blocks))] * 2
    block = (side, ow)
    return pl.pallas_call(
        functools.partial(layer_kernel, dims),
        out_shape=(
            jax.ShapeDtypeStruct((height, ow), BF),
            jax.ShapeDtypeStruct((height, width), BF),
            jax.ShapeDtypeStruct((depth, ow), F32),
        ),
        in_specs=[hbm, hbm, hbm, smem, smem, smem, hbm],
        out_specs=(vmem, vmem, vmem),
        scratch_shapes=[
            pltpu.VMEM((height, nz * width), BF),
            pltpu.VMEM((depth, nz * ow), BF),
            pltpu.VMEM((offs, slots, side, side), BF),
            pltpu.VMEM((height, ow), BF),
            pltpu.VMEM((offs, slots, side, side), BF),
            pltpu.VMEM((offs, slots, *block), F32),
            pltpu.VMEM((blocks, *block), F32),
            pltpu.VMEM((blocks, *block), BF),
            pltpu.VMEM((offs, blocks, *block), BF),
            pltpu.VMEM((offs, blocks, *block), BF),
            pltpu.VMEM((height, nz * ow), BF),
            pltpu.VMEM((depth, ow), BF),
            pltpu.VMEM((spare, blocks, *block), BF),
            pltpu.VMEM((spare, blocks, side, width), BF),
        ]
        + [pltpu.VMEM((blocks, *block), BF)] * offs
        + [pltpu.VMEM((f, depth // f, ow), BF) for f in factors]
        + [pltpu.VMEM((depth, ow), BF) for f in factors]
        + [dma((2, blocks)), dma((nz, blocks)), dma((nz, blocks)), dma((spare, nz, blocks))]
        + banded
        + banded
        + [dma((2, blocks)), dma((nz, blocks))]
        + [dma((spare, blocks)), dma((spare, blocks)), dma((blocks,))]
        + [dma((2, nz)), dma((nz, 2)), dma((1,)), dma((1,)), dma((4,))]
        + psems,
        compiler_params=pltpu.CompilerParams(
            collective_id=0, has_side_effects=True, vmem_limit_bytes=63 * 1024 * 1024
        ),
    )(x, w, tv, jnp.swapaxes(tr, 0, 1), jnp.swapaxes(tc, 0, 1), cnt, go)


def solution(mesh):
    return jax.shard_map(
        functools.partial(on_device, mesh.shape["blk"], mesh.shape["feat"]),
        mesh=mesh,
        in_specs=(
            P("blk", "feat"),
            P(None, "feat"),
            P("blk", None, None, None, None),
            P("blk", None, None),
            P("blk", None, None),
            P("blk", None),
            P("blk", "feat"),
        ),
        out_specs=(P("blk", "feat"), P("blk", "feat"), P(None, "feat")),
        check_vma=False,
    )
```

time: 83.7 us -> 66.1 us (0.79)
  Pallas kernels: 77.8 us -> 60.2 us
    pallas_call x1, Pallas kernels: 77.8 us -> 60.2 us  [on_device(): pl.pallas_call(functools.partial(layer_kernel, dims), out_shape=(jax.Shap...]
where the time goes in v1:
time: 66.1 us; the launch traced here: 65.9 us
  Pallas kernels  60.2 us (91%)
  local copies, waits for them, and re-layouts  5.01 us (8%)
    pallas_call x1, Pallas kernels, on_device(): pl.pallas_call(functools.partial(layer_kernel, dims), out_shape=(jax.Shap...  60.2 us
    unnamed x3, local copies, waits for them, and re-layouts  5.01 us

profile of v1, /device:TPU:0, one launch (start us, length us, event | category | flops | bytes accessed | tf_op | source)
XLA Modules:
  0.0 65.9 jit_solution(9780487983975680441)
XLA Ops:
  0.6 60.2 %shard_map.94 = (bf16[1024,128]{1,0:T(8,128)(2,1)}, bf16[1024,128]{1,0:T(8,128)(2,1)}, f32[512,128]{1,0:T(8,128)}) custom-call(bf16[1024,128]{1,0:T(8,128)(2,1)} %x.1, bf16[512,128]{1,0:T(8,128)(2,1)} %w_in.1, bf16[1,5,8,128,128]{4,3,2,1,0:T(8,128)(2,1)} %tv_in.1, s32[5,1,8]{2,1,0:T(1,128)} %bitcast.2, s32[5,1,8]{2,1,0:T(1,128)} %bitcast.3, s32[1,5]{1,0:T(1,128)} %cnt.1, ...), custom_call_target="tpu_custom_call" | custom-call | tf_op jit(solution)/shard_map/pallas_call | solution.py:540
  60.9 1.7 %copy.13 = bf16[1024,128]{1,0:T(8,128)(2,1)} copy(bf16[1024,128]{1,0:T(8,128)(2,1)} %get-tuple-element.6) | data formatting | bytes 524288
  62.5 1.7 %copy.14 = bf16[1024,128]{1,0:T(8,128)(2,1)} copy(bf16[1024,128]{1,0:T(8,128)(2,1)} %get-tuple-element.7) | data formatting | bytes 524288
  64.2 1.7 %copy.15 = f32[512,128]{1,0:T(8,128)} copy(f32[512,128]{1,0:T(8,128)} %get-tuple-element.8) | data formatting | bytes 524288

commit v2 on v1

--- a/solution.py
+++ b/solution.py
@@ -28,15 +28,15 @@
 
 
 def layer_kernel(
-    dims, x, w_in, tv_in, tr, tc, cnt, go_in, y, gx, gw,
-    xg, wg, tv, go, tt, prod, acc, gp, sent, got, gg, gwb, pe, ge, *rest
+    dims, x, w_in, tv_in, tr_in, tc_in, cnt_in, go_in, y, gx, gw,
+    tr, tc, cnt, xg, wg, tv, go, tt, prod, acc, gp, sent, got, gg, gwb, pe, ge, *rest
 ):
     nb, nz, offs, slots, blocks, side, width, ow, factors = dims
     stages = len(factors)
     hid, rest = rest[:offs], rest[offs:]
     gathered, summed = rest[:stages], rest[stages : 2 * stages]
-    (xs, xr, xl, xb, hs, hr, gs, gr, zs, zr, es, ges, ger, ws, wr, ks, kr, near) = rest[2 * stages : 2 * stages + 18]
-    psems = rest[2 * stages + 18 :]
+    (xs, xr, xe, xl, xb, hs, hr, hall, gs, gr, zs, zr, es, ges, ger, ws, wr, ks, kr, near) = rest[2 * stages : 2 * stages + 20]
+    psems = rest[2 * stages + 20 :]
     reach = (offs - 1) // 2
     half = nz // 2
     me = lax.axis_index("feat")
@@ -78,6 +78,9 @@
         pltpu.make_async_copy(x, xg.at[:, xcols(me)], near.at[1]),
         pltpu.make_async_copy(tv_in.at[0], tv, near.at[2]),
         pltpu.make_async_copy(go_in, go, near.at[3]),
+        pltpu.make_async_copy(tr_in, tr, near.at[4]),
+        pltpu.make_async_copy(tc_in, tc, near.at[5]),
+        pltpu.make_async_copy(cnt_in, cnt, near.at[6]),
     ]
     for copy in local:
         copy.start()
@@ -112,21 +115,26 @@
         return pl.ds(pl.multiple_of(piece * (depth // 2), depth // 2), depth // 2)
 
     def x_copy(way, b):
+        landed = xe.at[me, b - relayed[0]] if way == 0 and b in relayed else xr.at[b]
         return remote(
-            x.at[rows(b), :], xg.at[rows(b), xcols(me)], xs.at[way, b], xr.at[me, b], {"feat": (inner, other)[way]}
+            x.at[rows(b), :], xg.at[rows(b), xcols(me)], xs.at[way], landed, {"feat": (inner, other)[way]}
         )
 
     def x_relay(e, b):
         piece = xg.at[rows(b), xcols(e)]
-        return remote(piece, piece, xl.at[e, b], xr.at[e, b], {"feat": other})
+        return remote(piece, piece, xl.at[0], xr.at[b], {"feat": other})
 
     def x_back(s, e, j, b):
         piece = xg.at[rows(b), xcols(s)]
-        return remote(piece, piece, xb.at[j - 1, s, b], xr.at[s, b], {"feat": e})
-
-    def x_wait(s, b):
-        piece = xg.at[rows(b), xcols(s)]
-        remote(piece, piece, xl.at[s, b], xr.at[s, b], {"feat": other}).wait_recv()
+        return remote(piece, piece, xb.at[j - 1], xr.at[b], {"feat": e})
+
+    def x_early(e, b):
+        piece = xg.at[rows(b), xcols(e)]
+        remote(piece, piece, xl.at[0], xe.at[e, b - relayed[0]], {"feat": other}).wait_recv()
+
+    def x_wait(count, b):
+        piece = xg.at[rows(b), pl.ds(0, count * width)]
+        remote(piece, piece, xl.at[0], xr.at[b], {"feat": other}).wait_recv()
 
     def w_up():
         return remote(w_in.at[part_of(core), :], wg.at[part_of(core), ocols(me)], ws.at[0, 0], wr.at[me, core], {"feat": inner})
@@ -168,20 +176,24 @@
     landing = {PAIR: PAIR, AHEAD: BEHIND, BEHIND: AHEAD}
 
     def hid_copy(role, b):
-        return remote(hid[OWN].at[b], hid[landing[role]].at[b], hs.at[role, b], hr.at[landing[role], b], owner_at(role))
+        landed = hr.at[0, b] if role == BEHIND else hall.at[landing[role]]
+        return remote(hid[OWN].at[b], hid[landing[role]].at[b], hs.at[role], landed, owner_at(role))
 
     def hid_wait(role, b):
-        remote(hid[role].at[b], hid[role].at[b], hs.at[role, b], hr.at[role, b], owner_at(PAIR)).wait_recv()
+        remote(hid[role].at[b], hid[role].at[b], hs.at[role], hr.at[int(role == OWN), b], owner_at(PAIR)).wait_recv()
+
+    def hid_whole(role):
+        remote(hid[role], hid[role], hs.at[role], hall.at[role], owner_at(PAIR)).wait_recv()
 
     def hid_passed(b):
-        return remote(hid[AHEAD].at[b], hid[CROSS].at[b], hs.at[CROSS, b], hr.at[CROSS, b], owner_at(PAIR))
+        return remote(hid[AHEAD].at[b], hid[CROSS].at[b], hs.at[CROSS], hall.at[CROSS], owner_at(PAIR))
 
     def hid_relay(b):
         hid_wait(AHEAD, b)
         hid_passed(b).start()
 
     def hid_down(j, b):
-        return remote(pe.at[j - 1, b], hid[OWN].at[b], es.at[j - 1, b], hr.at[OWN, b], {"feat": end_at(j)})
+        return remote(pe.at[j - 1, b], hid[OWN].at[b], es.at[j - 1], hr.at[1, b], {"feat": end_at(j)})
 
     def spread(b):
         hid_copy(AHEAD, b).start()
@@ -200,7 +212,7 @@
             @pl.when(in_relay(b + 2))
             def _():
                 for j in ends:
-                    x_wait(end_at(j), b + 2)
+                    x_early(end_at(j), b + 2)
                     x_relay(end_at(j), b + 2).start()
 
         per_block = slots // blocks
@@ -211,12 +223,14 @@
 
         @pl.when(is_inner)
         def _():
-            for j in ends:
-                @pl.when(jnp.logical_not(in_relay(b)))
-                def _():
-                    x_wait(end_at(j), b)
-            for j in range(half):
-                x_wait(nz - 1 - end_at(j), b)
+            @pl.when(in_relay(b))
+            def _():
+                x_wait(half, b)
+
+            @pl.when(jnp.logical_not(in_relay(b)))
+            def _():
+                x_wait(nz - 1, b)
+
             hid[OWN][b] = jnp.dot(xg[rows(b), :], wg[:, ocols(me)], preferred_element_type=F32).astype(BF)
             spread(b)
 
@@ -245,6 +259,8 @@
         return carry
 
     lax.fori_loop(0, blocks, forward_step, 0)
+    for copy in local[4:]:
+        copy.wait()
 
     def forward_products(role):
         k = offset_of(role)
@@ -270,8 +286,7 @@
         lax.fori_loop(0, blocks, add, 0)
 
     gather_role(OWN)
-    for b in range(blocks):
-        hid_wait(PAIR, b)
+    hid_whole(PAIR)
     gather_role(PAIR)
     for b in range(max(blocks - lag, 0), blocks):
         hid_relay(b)
@@ -289,12 +304,10 @@
                         x_back(s, end_at(j), j, b).start()
 
     gather_role(AHEAD)
-    for b in range(blocks):
-        hid_wait(BEHIND, b)
+    hid_whole(BEHIND)
     gather_role(BEHIND)
     local[3].wait()
-    for b in range(blocks):
-        hid_wait(CROSS, b)
+    hid_whole(CROSS)
     forward_products(CROSS)
 
     def pointwise(b, carry):
@@ -323,18 +336,23 @@
 
     def sum_copy(role, c):
         return remote(
-            sent.at[role, c], got.at[arrives[role], c], gs.at[role, c], gr.at[arrives[role], c], owner_at(target[role])
+            sent.at[role, c], got.at[arrives[role], c], gs.at[role], gr.at[int(role == CROSS), c], owner_at(target[role])
         )
 
-    def sum_wait(role, c):
-        remote(got.at[role, c], got.at[role, c], gs.at[role, c], gr.at[role, c], owner_at(PAIR)).wait_recv()
+    def cross_wait(c):
+        piece = got.at[CROSS, c]
+        remote(piece, piece, gs.at[CROSS], gr.at[1, c], owner_at(PAIR)).wait_recv()
+
+    def sums_wait(c):
+        piece = got.at[pl.ds(0, 3), c]
+        remote(piece, piece, gs.at[PAIR], gr.at[0, c], owner_at(PAIR)).wait_recv()
 
     def send_sum(role, c):
         sent[role, c] = column_sum(role, c, None).astype(BF)
         sum_copy(role, c).start()
 
     def send_joint(c):
-        sum_wait(CROSS, c)
+        cross_wait(c)
         sent[AHEAD, c] = column_sum(AHEAD, c, got[CROSS, c].astype(F32)).astype(BF)
         sum_copy(AHEAD, c).start()
 
@@ -363,16 +381,16 @@
 
     def g_copy(way, b):
         piece = gg.at[rows(b), ocols(me)]
-        return remote(piece, piece, zs.at[way, b], zr.at[me, b], {"feat": (inner, other)[way]})
-
-    def g_wait(s, b):
-        piece = gg.at[rows(b), ocols(s)]
-        remote(piece, piece, zs.at[0, b], zr.at[s, b], {"feat": other}).wait_recv()
+        return remote(piece, piece, zs.at[way], zr.at[b], {"feat": (inner, other)[way]})
+
+    def g_wait(b):
+        piece = gg.at[rows(b), pl.ds(0, (nz - 1) * ow)]
+        remote(piece, piece, zs.at[0], zr.at[b], {"feat": other}).wait_recv()
 
     def make_grad(b):
         total = column_sum(OWN, b, gp[b].astype(F32))
+        sums_wait(b)
         for role in (PAIR, BEHIND, AHEAD):
-            sum_wait(role, b)
             total = total + got[role, b].astype(F32)
         grad = total.astype(BF)
         gg[rows(b), ocols(me)] = grad
@@ -381,13 +399,12 @@
         @pl.when(jnp.logical_not(is_inner))
         def _():
             g_copy(0, b).start()
-            for step in range(1, nz):
-                x_wait(lax.rem(me + step, nz), b)
+            x_wait(nz - 1, b)
 
         gw[...] += lax.dot_general(xg[rows(b), :], grad, (((0,), (0,)), ((), ())), preferred_element_type=F32)
 
     def gx_down(j, b):
-        return remote(ge.at[j - 1, b], gx.at[rows(b), :], ges.at[j - 1, b], ger.at[b], {"feat": end_at(j)})
+        return remote(ge.at[j - 1, b], gx.at[rows(b), :], ges.at[j - 1], ger.at[0], {"feat": end_at(j)})
 
     def finish(b):
         @pl.when(is_inner)
@@ -396,8 +413,7 @@
             def _():
                 w_swap(False).wait_recv()
 
-            for step in range(1, nz):
-                g_wait(lax.rem(me + step, nz), b)
+            g_wait(b)
 
             def grad_of(z):
                 return lax.dot_general(
@@ -435,7 +451,7 @@
 
         for step in range(1, size):
             _, there, peer = stage_peer(stage, step)
-            remote(src.at[part(there), :], buf.at[step], rs_s.at[step], rs_r.at[step], {"blk": peer}).start()
+            remote(src.at[part(there), :], buf.at[step - 1], rs_s.at[0], rs_r.at[0], {"blk": peer}).start()
         if stage == 0:
             for b in range(blocks - behind, blocks - 1):
                 finish(b)
@@ -444,70 +460,52 @@
             total = gw[part(digit), :]
         else:
             total = src[part(digit), :].astype(F32)
+        remote(buf, buf, rs_s.at[0], rs_r.at[0], owner_at(PAIR)).wait_recv()
         for step in range(1, size):
-            _, _, peer = stage_peer(stage, step)
-            remote(buf.at[step], buf.at[step], rs_s.at[step], rs_r.at[step], {"blk": peer}).wait_recv()
-            total = total + buf[step].astype(F32)
+            total = total + buf[step - 1].astype(F32)
         out[part(digit), :] = total.astype(BF)
         for step in range(1, size):
             _, _, peer = stage_peer(stage, step)
             piece = out.at[part(digit), :]
-            remote(piece, piece, ag_s.at[step], ag_r.at[step], {"blk": peer}).start()
+            remote(piece, piece, ag_s.at[0], ag_r.at[0], {"blk": peer}).start()
         if stage == 0:
             finish(blocks - 1)
-        for step in range(1, size):
-            _, there, peer = stage_peer(stage, size - step)
-            piece = out.at[part(there), :]
-            remote(piece, piece, ag_s.at[step], ag_r.at[step], {"blk": peer}).wait_recv()
+        piece = out.at[pl.ds(0, height - chunk), :]
+        remote(piece, piece, ag_s.at[0], ag_r.at[0], owner_at(PAIR)).wait_recv()
     gw[...] = (summed[-1] if stages else gwb)[...].astype(F32)
 
     for stage in range(stages):
-        size = factors[stage]
-        buf = gathered[stage]
+        buf, out = gathered[stage], summed[stage]
         rs_s, rs_r, ag_s, ag_r = psems[4 * stage : 4 * stage + 4]
-        for step in range(1, size):
-            _, _, peer = stage_peer(stage, step)
-            remote(buf.at[step], buf.at[step], rs_s.at[step], rs_r.at[step], {"blk": peer}).wait_send()
-            remote(buf.at[step], buf.at[step], ag_s.at[step], ag_r.at[step], {"blk": peer}).wait_send()
-
-    def drain(b, carry):
-        g_copy(1, b).wait_send()
-
-        @pl.when(is_inner)
-        def _():
-            x_copy(1, b).wait_send()
-            for j in ends:
-                @pl.when(in_relay(b))
-                def _():
-                    x_relay(end_at(j), b).wait_send()
-
-                hid_down(j, b).wait_send()
-                gx_down(j, b).wait_send()
-                for step in range(nz):
-                    s = lax.rem(me + step, nz)
-
-                    @pl.when(s != end_at(j))
-                    def _():
-                        x_back(s, end_at(j), j, b).wait_send()
-
-        @pl.when(jnp.logical_not(is_inner))
-        def _():
-            @pl.when(jnp.logical_not(in_relay(b)))
-            def _():
-                x_copy(1, b).wait_send()
-
-            x_copy(0, b).wait_send()
-            g_copy(0, b).wait_send()
-            remote(gx.at[rows(b), :], gx.at[rows(b), :], ges.at[0, b], ger.at[b], {"feat": inner}).wait_recv()
-
-        for role in (PAIR, AHEAD, BEHIND):
-            hid_copy(role, b).wait_send()
-        hid_passed(b).wait_send()
-        for role in (PAIR, CROSS, AHEAD, BEHIND):
-            sum_copy(role, b).wait_send()
-        return carry
-
-    lax.fori_loop(0, blocks, drain, 0)
+        remote(buf, buf, rs_s.at[0], rs_r.at[0], owner_at(PAIR)).wait_send()
+        piece = out.at[pl.ds(0, height - height // factors[stage]), :]
+        remote(piece, piece, ag_s.at[0], ag_r.at[0], owner_at(PAIR)).wait_send()
+
+    def sent_all(ref, sem):
+        remote(ref, ref, sem, ger.at[0], owner_at(PAIR)).wait_send()
+
+    sent_all(gg.at[:, ocols(me)], zs.at[1])
+
+    @pl.when(is_inner)
+    def _():
+        sent_all(x, xs.at[1])
+        if half > 1:
+            sent_all(xg.at[pl.ds(0, len(relayed) * side), pl.ds(0, (half - 1) * width)], xl.at[0])
+        for j in ends:
+            sent_all(pe.at[j - 1], es.at[j - 1])
+            sent_all(ge.at[j - 1], ges.at[j - 1])
+            sent_all(xg.at[:, pl.ds(0, (nz - 1) * width)], xb.at[j - 1])
+
+    @pl.when(jnp.logical_not(is_inner))
+    def _():
+        sent_all(x.at[pl.ds(0, (blocks - len(relayed)) * side), :], xs.at[1])
+        sent_all(x, xs.at[0])
+        sent_all(gg.at[:, ocols(me)], zs.at[0])
+        remote(gx, gx, ges.at[0], ger.at[0], {"feat": inner}).wait_recv()
+
+    for role in (PAIR, CROSS, AHEAD, BEHIND):
+        sent_all(hid[role], hs.at[role])
+        sent_all(sent.at[role], gs.at[role])
 
     @pl.when(is_inner)
     def _():
@@ -518,6 +516,16 @@
     @pl.when(jnp.logical_not(is_inner))
     def _():
         w_up().wait_send()
+
+
+def write_out(*refs):
+    count = (len(refs) - 1) // 2
+    done = refs[-1]
+    copies = [pltpu.make_async_copy(refs[i], refs[count + i], done.at[i]) for i in range(count)]
+    for copy in copies:
+        copy.start()
+    for copy in copies:
+        copy.wait()
 
 
 def on_device(nb, nz, x, w, tv, tr, tc, cnt, go):
@@ -530,23 +538,24 @@
     spare = max(nz // 2 - 1, 1)
     vmem = pl.BlockSpec(memory_space=pltpu.VMEM)
     hbm = pl.BlockSpec(memory_space=pltpu.HBM)
-    smem = pl.BlockSpec(memory_space=pltpu.SMEM)
     dma = pltpu.SemaphoreType.DMA
     psems = []
     for f in factors:
-        psems += [dma((f,))] * 4
-    banded = [dma((offs, blocks))] * 2
+        psems += [dma((1,))] * 4
     block = (side, ow)
-    return pl.pallas_call(
+    results = pl.pallas_call(
         functools.partial(layer_kernel, dims),
         out_shape=(
-            jax.ShapeDtypeStruct((height, ow), BF),
-            jax.ShapeDtypeStruct((height, width), BF),
-            jax.ShapeDtypeStruct((depth, ow), F32),
+            pltpu.VMEM((height, ow), BF),
+            pltpu.VMEM((height, width), BF),
+            pltpu.VMEM((depth, ow), F32),
         ),
-        in_specs=[hbm, hbm, hbm, smem, smem, smem, hbm],
+        in_specs=[hbm] * 7,
         out_specs=(vmem, vmem, vmem),
         scratch_shapes=[
+            pltpu.SMEM((offs, 1, slots), tr.dtype),
+            pltpu.SMEM((offs, 1, slots), tc.dtype),
+            pltpu.SMEM(cnt.shape, cnt.dtype),
             pltpu.VMEM((height, nz * width), BF),
             pltpu.VMEM((depth, nz * ow), BF),
             pltpu.VMEM((offs, slots, side, side), BF),
@@ -563,19 +572,26 @@
             pltpu.VMEM((spare, blocks, side, width), BF),
         ]
         + [pltpu.VMEM((blocks, *block), BF)] * offs
-        + [pltpu.VMEM((f, depth // f, ow), BF) for f in factors]
+        + [pltpu.VMEM((f - 1, depth // f, ow), BF) for f in factors]
         + [pltpu.VMEM((depth, ow), BF) for f in factors]
-        + [dma((2, blocks)), dma((nz, blocks)), dma((nz, blocks)), dma((spare, nz, blocks))]
-        + banded
-        + banded
-        + [dma((2, blocks)), dma((nz, blocks))]
-        + [dma((spare, blocks)), dma((spare, blocks)), dma((blocks,))]
-        + [dma((2, nz)), dma((nz, 2)), dma((1,)), dma((1,)), dma((4,))]
+        + [dma((2,)), dma((blocks,)), dma((nz, 2)), dma((1,)), dma((spare,))]
+        + [dma((offs,)), dma((2, blocks)), dma((offs,))]
+        + [dma((offs,)), dma((2, blocks))]
+        + [dma((2,)), dma((blocks,))]
+        + [dma((spare,)), dma((spare,)), dma((1,))]
+        + [dma((2, nz)), dma((nz, 2)), dma((1,)), dma((1,)), dma((7,))]
         + psems,
         compiler_params=pltpu.CompilerParams(
-            collective_id=0, has_side_effects=True, vmem_limit_bytes=63 * 1024 * 1024
+            collective_id=0, has_side_effects=True, vmem_limit_bytes=32 * 1024 * 1024
         ),
-    )(x, w, tv, jnp.swapaxes(tr, 0, 1), jnp.swapaxes(tc, 0, 1), cnt, go)
+    )(*[pltpu.with_memory_space_constraint(a, pltpu.HBM) for a in (x, w, tv, jnp.swapaxes(tr, 0, 1), jnp.swapaxes(tc, 0, 1), cnt, go)])
+    return pl.pallas_call(
+        write_out,
+        out_shape=tuple(jax.ShapeDtypeStruct(r.shape, r.dtype) for r in results),
+        in_specs=[vmem] * len(results),
+        out_specs=(hbm,) * len(results),
+        scratch_shapes=[dma((len(results),))],
+    )(*[pltpu.with_memory_space_constraint(r, pltpu.VMEM) for r in results])
 
 
 def solution(mesh):

time: 66.1 us -> 57.3 us (0.87)
  local copies, waits for them, and re-layouts: 5.01 us -> 0 us
  Pallas kernels: 60.2 us -> 56.5 us
    unnamed x3 -> x0, local copies, waits for them, and re-layouts: 5.01 us -> none
    pallas_call x1 -> x2, Pallas kernels: 60.2 us -> 56.5 us  [the longest x1 55.6 us: on_device(): pl.pallas_call(functools.partial(layer_kernel, dims), out_shape=(pltpu.VM...]
where the time goes in v2:
time: 57.3 us; the launch traced here: 57.2 us
  Pallas kernels  56.5 us (99%)
  between operations  0.64 us (1%)
    pallas_call x1, Pallas kernels, on_device(): pl.pallas_call(functools.partial(layer_kernel, dims), out_shape=(pltpu.VM...  55.6 us

profile of v2, /device:TPU:0, one launch (start us, length us, event | category | flops | bytes accessed | tf_op | source)
XLA Modules:
  0.0 57.2 jit_solution(15691558821286230904)
XLA Ops:
  0.6 55.6 %shard_map.94 = (bf16[1024,128]{1,0:T(8,128)(2,1)S(1)}, bf16[1024,128]{1,0:T(8,128)(2,1)S(1)}, f32[512,128]{1,0:T(8,128)S(1)}) custom-call(bf16[1024,128]{1,0:T(8,128)(2,1)} %x.1, bf16[512,128]{1,0:T(8,128)(2,1)} %w_in.1, bf16[1,5,8,128,128]{4,3,2,1,0:T(8,128)(2,1)} %tv_in.1, s32[5,1,8]{2,1,0:T(1,128)} %bitcast.2, s32[5,1,8]{2,1,0:T(1,128)} %bitcast.3, ...), custom_call_target="tpu_custom_call" | custom-call | tf_op jit(solution)/shard_map/pallas_call | solution.py:546
  56.3 0.9 %shard_map.95 = (bf16[1024,128]{1,0:T(8,128)(2,1)}, bf16[1024,128]{1,0:T(8,128)(2,1)}, f32[512,128]{1,0:T(8,128)}) custom-call(bf16[1024,128]{1,0:T(8,128)(2,1)S(1)} %get-tuple-element.6.refs_0_, bf16[1024,128]{1,0:T(8,128)(2,1)S(1)} %get-tuple-element.7.refs_1_, f32[512,128]{1,0:T(8,128)S(1)} %get-tuple-element.8.refs_2_), custom_call_target="tpu_custom_call" | custom-call | tf_op jit(solution)/shard_map/pallas_call | solution.py:588

commit v3 on v2

--- a/solution.py
+++ b/solution.py
@@ -35,8 +35,8 @@
     stages = len(factors)
     hid, rest = rest[:offs], rest[offs:]
     gathered, summed = rest[:stages], rest[stages : 2 * stages]
-    (xs, xr, xe, xl, xb, hs, hr, hall, gs, gr, zs, zr, es, ges, ger, ws, wr, ks, kr, near) = rest[2 * stages : 2 * stages + 20]
-    psems = rest[2 * stages + 20 :]
+    (xs, xr, xb, hs, hr, hall, gs, gr, zs, zr, es, ges, ger, ws, wr, ks, kr, near) = rest[2 * stages : 2 * stages + 18]
+    psems = rest[2 * stages + 18 :]
     reach = (offs - 1) // 2
     half = nz // 2
     me = lax.axis_index("feat")
@@ -50,13 +50,9 @@
     other = nz - 1 - inner
     is_inner = me == inner
     ends = range(1, half)
-    relayed = (blocks // 2 - 1, blocks // 2)
 
     def end_at(j):
         return jnp.where(lower, half - 1 - j, half + j)
-
-    def in_relay(b):
-        return (b >= relayed[0]) & (b <= relayed[1])
 
     def offset_of(role):
         return reach + lean[role] * turn
@@ -115,26 +111,17 @@
         return pl.ds(pl.multiple_of(piece * (depth // 2), depth // 2), depth // 2)
 
     def x_copy(way, b):
-        landed = xe.at[me, b - relayed[0]] if way == 0 and b in relayed else xr.at[b]
         return remote(
-            x.at[rows(b), :], xg.at[rows(b), xcols(me)], xs.at[way], landed, {"feat": (inner, other)[way]}
+            x.at[rows(b), :], xg.at[rows(b), xcols(me)], xs.at[way], xr.at[b], {"feat": (inner, other)[way]}
         )
-
-    def x_relay(e, b):
-        piece = xg.at[rows(b), xcols(e)]
-        return remote(piece, piece, xl.at[0], xr.at[b], {"feat": other})
 
     def x_back(s, e, j, b):
         piece = xg.at[rows(b), xcols(s)]
         return remote(piece, piece, xb.at[j - 1], xr.at[b], {"feat": e})
 
-    def x_early(e, b):
-        piece = xg.at[rows(b), xcols(e)]
-        remote(piece, piece, xl.at[0], xe.at[e, b - relayed[0]], {"feat": other}).wait_recv()
-
-    def x_wait(count, b):
-        piece = xg.at[rows(b), pl.ds(0, count * width)]
-        remote(piece, piece, xl.at[0], xr.at[b], {"feat": other}).wait_recv()
+    def x_wait(b):
+        piece = xg.at[rows(b), pl.ds(0, (nz - 1) * width)]
+        remote(piece, piece, xs.at[0], xr.at[b], {"feat": other}).wait_recv()
 
     def w_up():
         return remote(w_in.at[part_of(core), :], wg.at[part_of(core), ocols(me)], ws.at[0, 0], wr.at[me, core], {"feat": inner})
@@ -164,8 +151,7 @@
     @pl.when(jnp.logical_not(is_inner))
     def _():
         for b in range(blocks):
-            if b not in relayed:
-                x_copy(1, b).start()
+            x_copy(1, b).start()
             x_copy(0, b).start()
             if b == 0:
                 w_up().start()
@@ -196,11 +182,20 @@
         return remote(pe.at[j - 1, b], hid[OWN].at[b], es.at[j - 1], hr.at[1, b], {"feat": end_at(j)})
 
     def spread(b):
+        hid_copy(PAIR, b).start()
         hid_copy(AHEAD, b).start()
         hid_copy(BEHIND, b).start()
-        hid_copy(PAIR, b).start()
-
-    lag = 2
+
+    def hidden_of(z, b):
+        return jnp.dot(xg[rows(b), :], wg[:, ocols(z)], preferred_element_type=F32).astype(BF)
+
+    def serve_ends(b):
+        for j in ends:
+            pe[j - 1, b] = hidden_of(end_at(j), b)
+            hid_down(j, b).start()
+            x_back(me, end_at(j), j, b).start()
+
+    lag = 4
 
     def forward_step(b, carry):
         @pl.when(is_inner)
@@ -209,12 +204,6 @@
             def _():
                 x_copy(1, b + 4).start()
 
-            @pl.when(in_relay(b + 2))
-            def _():
-                for j in ends:
-                    x_early(end_at(j), b + 2)
-                    x_relay(end_at(j), b + 2).start()
-
         per_block = slots // blocks
         for role in range(offs):
             for s in range(per_block):
@@ -223,15 +212,13 @@
 
         @pl.when(is_inner)
         def _():
-            @pl.when(in_relay(b))
+            x_wait(b)
+
+            @pl.when(b >= 1)
             def _():
-                x_wait(half, b)
-
-            @pl.when(jnp.logical_not(in_relay(b)))
-            def _():
-                x_wait(nz - 1, b)
-
-            hid[OWN][b] = jnp.dot(xg[rows(b), :], wg[:, ocols(me)], preferred_element_type=F32).astype(BF)
+                serve_ends(b)
+
+            hid[OWN][b] = hidden_of(me, b)
             spread(b)
 
             @pl.when(b == 0)
@@ -241,11 +228,7 @@
                     w_across(end_at(j)).start()
                 for j in ends:
                     w_wait(end_at(j), 1 - core)
-
-            for j in ends:
-                pe[j - 1, b] = jnp.dot(xg[rows(b), :], wg[:, ocols(end_at(j))], preferred_element_type=F32).astype(BF)
-                hid_down(j, b).start()
-                x_back(me, end_at(j), j, b).start()
+                serve_ends(0)
 
         @pl.when(jnp.logical_not(is_inner))
         def _():
@@ -399,7 +382,7 @@
         @pl.when(jnp.logical_not(is_inner))
         def _():
             g_copy(0, b).start()
-            x_wait(nz - 1, b)
+            x_wait(b)
 
         gw[...] += lax.dot_general(xg[rows(b), :], grad, (((0,), (0,)), ((), ())), preferred_element_type=F32)
 
@@ -425,19 +408,7 @@
                 gx_down(j, b).start()
             gx[rows(b), :] = grad_of(me)
 
-    behind = 3
-
-    def backward_step(c, carry):
-        make_grad(c)
-
-        @pl.when(c >= behind)
-        def _():
-            finish(c - behind)
-
-        return carry
-
-    lax.fori_loop(0, blocks, backward_step, 0)
-
+    loop(make_grad)
     gwb[...] = gw[...].astype(BF)
     height = gw.shape[0]
     for stage in range(stages):
@@ -453,7 +424,7 @@
             _, there, peer = stage_peer(stage, step)
             remote(src.at[part(there), :], buf.at[step - 1], rs_s.at[0], rs_r.at[0], {"blk": peer}).start()
         if stage == 0:
-            for b in range(blocks - behind, blocks - 1):
+            for b in range(blocks - 2):
                 finish(b)
         digit, _, _ = stage_peer(stage, 1)
         if stage == 0:
@@ -469,7 +440,8 @@
             piece = out.at[part(digit), :]
             remote(piece, piece, ag_s.at[0], ag_r.at[0], {"blk": peer}).start()
         if stage == 0:
-            finish(blocks - 1)
+            for b in range(max(blocks - 2, 0), blocks):
+                finish(b)
         piece = out.at[pl.ds(0, height - chunk), :]
         remote(piece, piece, ag_s.at[0], ag_r.at[0], owner_at(PAIR)).wait_recv()
     gw[...] = (summed[-1] if stages else gwb)[...].astype(F32)
@@ -489,8 +461,6 @@
     @pl.when(is_inner)
     def _():
         sent_all(x, xs.at[1])
-        if half > 1:
-            sent_all(xg.at[pl.ds(0, len(relayed) * side), pl.ds(0, (half - 1) * width)], xl.at[0])
         for j in ends:
             sent_all(pe.at[j - 1], es.at[j - 1])
             sent_all(ge.at[j - 1], ges.at[j - 1])
@@ -498,7 +468,7 @@
 
     @pl.when(jnp.logical_not(is_inner))
     def _():
-        sent_all(x.at[pl.ds(0, (blocks - len(relayed)) * side), :], xs.at[1])
+        sent_all(x, xs.at[1])
         sent_all(x, xs.at[0])
         sent_all(gg.at[:, ocols(me)], zs.at[0])
         remote(gx, gx, ges.at[0], ger.at[0], {"feat": inner}).wait_recv()
@@ -574,7 +544,7 @@
         + [pltpu.VMEM((blocks, *block), BF)] * offs
         + [pltpu.VMEM((f - 1, depth // f, ow), BF) for f in factors]
         + [pltpu.VMEM((depth, ow), BF) for f in factors]
-        + [dma((2,)), dma((blocks,)), dma((nz, 2)), dma((1,)), dma((spare,))]
+        + [dma((2,)), dma((blocks,)), dma((spare,))]
         + [dma((offs,)), dma((2, blocks)), dma((offs,))]
         + [dma((offs,)), dma((2, blocks))]
         + [dma((2,)), dma((blocks,))]

time: 57.3 us -> 54.9 us (0.958)
  Pallas kernels: 56.5 us -> 54.1 us
    pallas_call x1, Pallas kernels: 55.6 us -> 53.2 us  [on_device(): pl.pallas_call(functools.partial(layer_kernel, dims), out_shape=(pltpu.VM...]
where the time goes in v3:
time: 54.9 us; the launch traced here: 54.7 us
  Pallas kernels  54.1 us (99%)
  between operations  0.64 us (1%)
    pallas_call x1, Pallas kernels, on_device(): pl.pallas_call(functools.partial(layer_kernel, dims), out_shape=(pltpu.VM...  53.2 us

profile of v3, /device:TPU:0, one launch (start us, length us, event | category | flops | bytes accessed | tf_op | source)
XLA Modules:
  0.0 54.7 jit_solution(12661620839444433994)
XLA Ops:
  0.6 53.2 %shard_map.94 = (bf16[1024,128]{1,0:T(8,128)(2,1)S(1)}, bf16[1024,128]{1,0:T(8,128)(2,1)S(1)}, f32[512,128]{1,0:T(8,128)S(1)}) custom-call(bf16[1024,128]{1,0:T(8,128)(2,1)} %x.1, bf16[512,128]{1,0:T(8,128)(2,1)} %w_in.1, bf16[1,5,8,128,128]{4,3,2,1,0:T(8,128)(2,1)} %tv_in.1, s32[5,1,8]{2,1,0:T(1,128)} %bitcast.2, s32[5,1,8]{2,1,0:T(1,128)} %bitcast.3, ...), custom_call_target="tpu_custom_call" | custom-call | tf_op jit(solution)/shard_map/pallas_call | solution.py:516
  53.8 0.9 %shard_map.95 = (bf16[1024,128]{1,0:T(8,128)(2,1)}, bf16[1024,128]{1,0:T(8,128)(2,1)}, f32[512,128]{1,0:T(8,128)}) custom-call(bf16[1024,128]{1,0:T(8,128)(2,1)S(1)} %get-tuple-element.6.refs_0_, bf16[1024,128]{1,0:T(8,128)(2,1)S(1)} %get-tuple-element.7.refs_1_, f32[512,128]{1,0:T(8,128)S(1)} %get-tuple-element.8.refs_2_), custom_call_target="tpu_custom_call" | custom-call | tf_op jit(solution)/shard_map/pallas_call | solution.py:558

commit v4 on v3

--- a/solution.py
+++ b/solution.py
@@ -29,14 +29,14 @@
 
 def layer_kernel(
     dims, x, w_in, tv_in, tr_in, tc_in, cnt_in, go_in, y, gx, gw,
-    tr, tc, cnt, xg, wg, tv, go, tt, prod, acc, gp, sent, got, gg, gwb, pe, ge, *rest
+    tr, tc, cnt, xg, wg, tv, go, tt, prod, acc, gp, sent, got, gg, gwb, pe, ge, wt, *rest
 ):
     nb, nz, offs, slots, blocks, side, width, ow, factors = dims
     stages = len(factors)
-    hid, rest = rest[:offs], rest[offs:]
+    hid, hid_far, rest = rest[:3], rest[3], rest[4:]
     gathered, summed = rest[:stages], rest[stages : 2 * stages]
-    (xs, xr, xb, hs, hr, hall, gs, gr, zs, zr, es, ges, ger, ws, wr, ks, kr, near) = rest[2 * stages : 2 * stages + 18]
-    psems = rest[2 * stages + 18 :]
+    (xs, xr, xb, hs, hr, hf, hall, gs, gr, zs, zr, zl, ze, es, ges, ger, ws, wr, ks, kr, near) = rest[2 * stages : 2 * stages + 21]
+    psems = rest[2 * stages + 21 :]
     reach = (offs - 1) // 2
     half = nz // 2
     me = lax.axis_index("feat")
@@ -50,6 +50,10 @@
     other = nz - 1 - inner
     is_inner = me == inner
     ends = range(1, half)
+    mine = jnp.where(lower, half - 1 - me, me - half)
+    straight = min(3, blocks)
+    passed = blocks // 2
+    wound = blocks // 2
 
     def end_at(j):
         return jnp.where(lower, half - 1 - j, half + j)
@@ -59,6 +63,16 @@
 
     def owner_at(role):
         return {"blk": lax.rem(own + lean[role] * turn + nb, nb)}
+
+    chip = own // 2
+    ahead_near = lax.rem(chip + own, 2) == 0
+    near_role = jnp.where(ahead_near, AHEAD, BEHIND)
+    far_role = AHEAD + BEHIND - near_role
+    near_lean = jnp.where(ahead_near, lean[AHEAD], lean[BEHIND]) * turn
+    near_owner = {"blk": lax.rem(own + near_lean + nb, nb)}
+    skip = 2 * lean[AHEAD] * (2 * lax.rem(chip, 2) - 1)
+    side_owner = {"blk": lax.rem(own + skip + nb, nb)}
+    side_source = {"blk": lax.rem(own - skip + nb, nb)}
 
     def rows(b):
         return pl.ds(pl.multiple_of(b * side, side), side)
@@ -95,8 +109,9 @@
     for step in range(1, nz):
         pl.semaphore_signal(barrier, inc=1, device_id={"feat": lax.rem(me + step, nz)}, device_id_type=MESH)
         greeted += 1
-    for role in (PAIR, AHEAD, BEHIND) if stages > 1 else ():
-        pl.semaphore_signal(barrier, inc=1, device_id=owner_at(role), device_id_type=MESH)
+    around = [owner_at(PAIR), owner_at(AHEAD), owner_at(BEHIND), side_owner, side_source]
+    for peer in around if stages > 1 else ():
+        pl.semaphore_signal(barrier, inc=1, device_id=peer, device_id_type=MESH)
         greeted += 1
     for stage in range(stages):
         for step in range(1, factors[stage]):
@@ -107,8 +122,12 @@
 
     depth = w_in.shape[0]
 
-    def part_of(piece):
-        return pl.ds(pl.multiple_of(piece * (depth // 2), depth // 2), depth // 2)
+    group = factors[0] if stages else 1
+
+    def part_of(digit):
+        return pl.ds(pl.multiple_of(digit * (depth // group), depth // group), depth // group)
+
+    my_part = part_of(stage_peer(0, 0)[0] if stages else 0)
 
     def x_copy(way, b):
         return remote(
@@ -124,15 +143,21 @@
         remote(piece, piece, xs.at[0], xr.at[b], {"feat": other}).wait_recv()
 
     def w_up():
-        return remote(w_in.at[part_of(core), :], wg.at[part_of(core), ocols(me)], ws.at[0, 0], wr.at[me, core], {"feat": inner})
-
-    def w_across(e):
-        piece = wg.at[part_of(core), ocols(e)]
-        return remote(piece, piece, ws.at[1, e], wr.at[e, core], owner_at(PAIR))
-
-    def w_wait(e, piece):
-        ref = wg.at[part_of(piece), ocols(e)]
-        remote(ref, ref, ws.at[1, e], wr.at[e, piece], owner_at(PAIR)).wait_recv()
+        return remote(w_in.at[my_part, :], wg.at[my_part, ocols(me)], ws.at[0], wr.at[mine - 1, 0], {"feat": inner})
+
+    def w_around(j):
+        piece = wg.at[my_part, ocols(end_at(j))]
+        remote(piece, piece, ws.at[j], wr.at[j - 1, 0], owner_at(PAIR)).wait_recv()
+        for step in range(1, group):
+            peer = {"blk": stage_peer(0, step)[2]}
+            remote(piece, piece, ws.at[j], wr.at[j - 1, 1], peer).start()
+
+    def w_rest(j):
+        return wg.at[pl.ds(0, depth - depth // group), ocols(end_at(j))]
+
+    def w_wait(j):
+        if group > 1:
+            remote(w_rest(j), w_rest(j), ws.at[j], wr.at[j - 1, 1], owner_at(PAIR)).wait_recv()
 
     def w_swap(sending):
         there = jnp.where(lower, half, 0)
@@ -145,46 +170,80 @@
 
     @pl.when(is_inner)
     def _():
-        for b in range(min(4, blocks)):
+        for b in range(min(6, blocks)):
             x_copy(1, b).start()
 
     @pl.when(jnp.logical_not(is_inner))
     def _():
         for b in range(blocks):
             x_copy(1, b).start()
+            if b == 0 and half > 1:
+                w_up().start()
             x_copy(0, b).start()
-            if b == 0:
-                w_up().start()
 
     for copy in local[:3]:
         copy.wait()
 
-    landing = {PAIR: PAIR, AHEAD: BEHIND, BEHIND: AHEAD}
-
-    def hid_copy(role, b):
-        landed = hr.at[0, b] if role == BEHIND else hall.at[landing[role]]
-        return remote(hid[OWN].at[b], hid[landing[role]].at[b], hs.at[role], landed, owner_at(role))
-
-    def hid_wait(role, b):
-        remote(hid[role].at[b], hid[role].at[b], hs.at[role], hr.at[int(role == OWN), b], owner_at(PAIR)).wait_recv()
+    near_slot = jnp.where(ahead_near, 0, 1)
+    far_slot = 1 - near_slot
+
+    def hid_pair(b):
+        return remote(hid[OWN].at[b], hid[PAIR].at[b], hs.at[PAIR], hall.at[PAIR], owner_at(PAIR))
+
+    def hid_straight(role, b):
+        slot = int(role == AHEAD)
+        return remote(hid[OWN].at[b], hid_far.at[slot, b], hs.at[role], hf.at[slot, b], owner_at(role))
+
+    def hid_near(b):
+        return remote(hid[OWN].at[b], hid_far.at[far_slot, b], hs.at[OWN], hf.at[far_slot, b], near_owner)
+
+    def hid_side(b):
+        return remote(
+            hid_far.at[near_slot, b], hid_far.at[far_slot, b], hs.at[offs], hf.at[far_slot, b], side_source
+        )
+
+    def hid_passed(b):
+        return remote(hid_far.at[0, b], hid[CROSS].at[b], hs.at[CROSS], hall.at[CROSS], owner_at(PAIR))
+
+    def hid_landed(slot, b):
+        piece = hid_far.at[slot, b]
+        remote(piece, piece, hs.at[OWN], hf.at[slot, b], owner_at(PAIR)).wait_recv()
 
     def hid_whole(role):
         remote(hid[role], hid[role], hs.at[role], hall.at[role], owner_at(PAIR)).wait_recv()
 
-    def hid_passed(b):
-        return remote(hid[AHEAD].at[b], hid[CROSS].at[b], hs.at[CROSS], hall.at[CROSS], owner_at(PAIR))
-
-    def hid_relay(b):
-        hid_wait(AHEAD, b)
-        hid_passed(b).start()
+    def take_near(b):
+        hid_landed(near_slot, b)
+
+        @pl.when(b < wound)
+        def _():
+            hid_side(b).start()
+
+        @pl.when(ahead_near)
+        def _():
+            hid_passed(b).start()
+
+    def take_far(b):
+        hid_landed(far_slot, b)
+
+        @pl.when(jnp.logical_not(ahead_near))
+        def _():
+            hid_passed(b).start()
 
     def hid_down(j, b):
-        return remote(pe.at[j - 1, b], hid[OWN].at[b], es.at[j - 1], hr.at[1, b], {"feat": end_at(j)})
+        return remote(pe.at[j - 1, b], hid[OWN].at[b], es.at[j - 1], hr.at[b], {"feat": end_at(j)})
 
     def spread(b):
-        hid_copy(PAIR, b).start()
-        hid_copy(AHEAD, b).start()
-        hid_copy(BEHIND, b).start()
+        hid_pair(b).start()
+
+        @pl.when(b < wound)
+        def _():
+            hid_near(b).start()
+
+        @pl.when(b >= wound)
+        def _():
+            hid_straight(AHEAD, b).start()
+            hid_straight(BEHIND, b).start()
 
     def hidden_of(z, b):
         return jnp.dot(xg[rows(b), :], wg[:, ocols(z)], preferred_element_type=F32).astype(BF)
@@ -193,16 +252,16 @@
         for j in ends:
             pe[j - 1, b] = hidden_of(end_at(j), b)
             hid_down(j, b).start()
-            x_back(me, end_at(j), j, b).start()
-
-    lag = 4
+
+    lag = min(3, blocks)
+    first = min(2, blocks - 1)
 
     def forward_step(b, carry):
         @pl.when(is_inner)
         def _():
-            @pl.when(b + 4 < blocks)
+            @pl.when(b + 6 < blocks)
             def _():
-                x_copy(1, b + 4).start()
+                x_copy(1, b + 6).start()
 
         per_block = slots // blocks
         for role in range(offs):
@@ -214,80 +273,87 @@
         def _():
             x_wait(b)
 
-            @pl.when(b >= 1)
+            @pl.when(b > first)
             def _():
                 serve_ends(b)
 
             hid[OWN][b] = hidden_of(me, b)
             spread(b)
 
-            @pl.when(b == 0)
+            @pl.when(b == first)
             def _():
                 for j in ends:
-                    w_wait(end_at(j), core)
-                    w_across(end_at(j)).start()
-                for j in ends:
-                    w_wait(end_at(j), 1 - core)
-                serve_ends(0)
+                    w_wait(j)
+                for early in range(first + 1):
+                    serve_ends(early)
 
         @pl.when(jnp.logical_not(is_inner))
         def _():
-            hid_wait(OWN, b)
+            remote(hid[OWN].at[b], hid[OWN].at[b], es.at[0], hr.at[b], {"feat": inner}).wait_recv()
             spread(b)
 
         @pl.when(b >= lag)
         def _():
-            hid_relay(b - lag)
+            take_near(b - lag)
 
         return carry
 
+    @pl.when(is_inner)
+    def _():
+        for j in ends:
+            w_around(j)
+
     lax.fori_loop(0, blocks, forward_step, 0)
-    for copy in local[4:]:
-        copy.wait()
-
-    def forward_products(role):
-        k = offset_of(role)
-        for s in range(slots):
-            prod[role, s] = jnp.dot(tv[k, s], hid[role][tc[k, 0, s]], preferred_element_type=F32)
-
-    def weight_of(table, k, s, b):
-        return jnp.where((table[k, 0, s] == b) & (s < cnt[0, k]), 1.0, 0.0).astype(F32)
-
-    def row_sum(role, b, total):
-        for s in range(slots):
-            total = total + prod[role, s] * weight_of(tr, offset_of(role), s, b)
-        return total
-
-    def gather_role(role):
-        forward_products(role)
-
-        def add(b, carry):
-            start = hid[OWN][b].astype(F32) if role == OWN else acc[b]
-            acc[b] = row_sum(role, b, start)
-            return carry
-
-        lax.fori_loop(0, blocks, add, 0)
-
-    gather_role(OWN)
-    hid_whole(PAIR)
-    gather_role(PAIR)
-    for b in range(max(blocks - lag, 0), blocks):
-        hid_relay(b)
 
     @pl.when(is_inner)
     def _():
         w_swap(True).start()
         for j in ends:
             for b in range(blocks):
-                for step in range(1, nz):
+                for step in range(nz):
                     s = lax.rem(me + step, nz)
 
                     @pl.when(s != end_at(j))
                     def _():
                         x_back(s, end_at(j), j, b).start()
 
+    for copy in local[4:]:
+        copy.wait()
+
+    def forward_products(role):
+        k = offset_of(role)
+        for s in range(slots):
+            c = tc[k, 0, s]
+            source = hid[role][c] if role < AHEAD else hid_far[role - AHEAD, c]
+            prod[role, s] = jnp.dot(tv[k, s], source, preferred_element_type=F32)
+
+    def weight_of(table, k, s, b):
+        return jnp.where((table[k, 0, s] == b) & (s < cnt[0, k]), 1.0, 0.0).astype(F32)
+
+    def row_sum(role, b, total):
+        for s in range(slots):
+            total = total + prod[role, s] * weight_of(tr, offset_of(role), s, b)
+        return total
+
+    def gather_role(role):
+        forward_products(role)
+
+        def add(b, carry):
+            start = hid[OWN][b].astype(F32) if role == OWN else acc[b]
+            acc[b] = row_sum(role, b, start)
+            return carry
+
+        lax.fori_loop(0, blocks, add, 0)
+
+    gather_role(OWN)
+    hid_whole(PAIR)
+    gather_role(PAIR)
+    for b in range(max(blocks - lag, 0), blocks):
+        take_near(b)
+    for b in range(blocks):
+        take_far(b)
+
     gather_role(AHEAD)
-    hid_whole(BEHIND)
     gather_role(BEHIND)
     local[3].wait()
     hid_whole(CROSS)
@@ -307,10 +373,10 @@
         for s in range(slots):
             prod[role, s] = jnp.dot(tt[role, s], gp[tr[offset_of(role), 0, s]], preferred_element_type=F32)
 
-    def column_sum(role, c, start):
+    def column_sum(role, offset, c, start):
         total = start
         for s in range(slots):
-            term = prod[role, s] * weight_of(tc, offset_of(role), s, c)
+            term = prod[role, s] * weight_of(tc, offset, s, c)
             total = term if total is None else total + term
         return total
 
@@ -326,89 +392,129 @@
         piece = got.at[CROSS, c]
         remote(piece, piece, gs.at[CROSS], gr.at[1, c], owner_at(PAIR)).wait_recv()
 
-    def sums_wait(c):
-        piece = got.at[pl.ds(0, 3), c]
-        remote(piece, piece, gs.at[PAIR], gr.at[0, c], owner_at(PAIR)).wait_recv()
-
     def send_sum(role, c):
-        sent[role, c] = column_sum(role, c, None).astype(BF)
+        sent[role, c] = column_sum(role, offset_of(role), c, None).astype(BF)
         sum_copy(role, c).start()
 
     def send_joint(c):
         cross_wait(c)
-        sent[AHEAD, c] = column_sum(AHEAD, c, got[CROSS, c].astype(F32)).astype(BF)
+        start = got[CROSS, c].astype(F32)
+        sent[AHEAD, c] = column_sum(AHEAD, offset_of(AHEAD), c, start).astype(BF)
         sum_copy(AHEAD, c).start()
 
-    def loop(step):
+    crossing_near = jnp.where(ahead_near, 1.0, 0.0).astype(F32)
+
+    def send_side(c):
+        cross_wait(c)
+        start = got[CROSS, c].astype(F32) * (1.0 - crossing_near)
+        sent[far_role, c] = column_sum(far_role, reach - near_lean, c, start).astype(BF)
+        remote(sent.at[far_role, c], got.at[OWN, c], gs.at[OWN], gr.at[2, c], side_owner).start()
+
+    def send_near(c):
+        start = got[CROSS, c].astype(F32) * crossing_near
+        total = column_sum(near_role, reach + near_lean, c, start)
+        piece = got.at[OWN, c]
+        remote(piece, piece, gs.at[OWN], gr.at[2, c], side_owner).wait_recv()
+        sent[near_role, c] = (total + got[OWN, c].astype(F32)).astype(BF)
+        remote(sent.at[near_role, c], got.at[AHEAD, c], gs.at[offs], gr.at[0, c], near_owner).start()
+
+    def loop(low, high, step):
         def body(c, carry):
             step(c)
             return carry
 
-        lax.fori_loop(0, blocks, body, 0)
+        lax.fori_loop(low, high, body, 0)
 
     backward_products(CROSS)
-    loop(lambda c: send_sum(CROSS, c))
+    loop(0, blocks, lambda c: send_sum(CROSS, c))
     backward_products(BEHIND)
+    for c in range(straight):
+        send_sum(BEHIND, c)
     backward_products(AHEAD)
-
-    def send_far(c):
-        send_sum(BEHIND, c)
+    for c in range(straight):
         send_joint(c)
-
-    loop(send_far)
+    loop(straight, blocks, send_side)
     backward_products(PAIR)
-    loop(lambda c: send_sum(PAIR, c))
+    loop(0, blocks, lambda c: send_sum(PAIR, c))
     backward_products(OWN)
 
     gw[...] = jnp.zeros_like(gw)
 
-    def g_copy(way, b):
+    def g_copy(way, b, landed):
         piece = gg.at[rows(b), ocols(me)]
-        return remote(piece, piece, zs.at[way], zr.at[b], {"feat": (inner, other)[way]})
+        return remote(piece, piece, zs.at[way], landed, {"feat": (inner, other)[way]})
 
     def g_wait(b):
-        piece = gg.at[rows(b), pl.ds(0, (nz - 1) * ow)]
+        piece = gg.at[rows(b), pl.ds(0, (half if b < passed else nz - 1) * ow)]
         remote(piece, piece, zs.at[0], zr.at[b], {"feat": other}).wait_recv()
 
-    def make_grad(b):
-        total = column_sum(OWN, b, gp[b].astype(F32))
-        sums_wait(b)
-        for role in (PAIR, BEHIND, AHEAD):
+    def g_pass(b):
+        for j in ends:
+            piece = gg.at[rows(b), ocols(end_at(j))]
+            remote(piece, piece, zl.at[0], ze.at[j - 1, b], {"feat": other}).wait_recv()
+            remote(piece, piece, zl.at[0], zr.at[b], {"feat": other}).start()
+
+    def make_grad(b, two):
+        pieces = got.at[pl.ds(0, 3 if two else 2), b]
+        total = column_sum(OWN, reach, b, gp[b].astype(F32))
+        remote(pieces, pieces, gs.at[PAIR], gr.at[0, b], owner_at(PAIR)).wait_recv()
+        for role in (PAIR, AHEAD, BEHIND)[: 3 if two else 2]:
             total = total + got[role, b].astype(F32)
         grad = total.astype(BF)
         gg[rows(b), ocols(me)] = grad
-        g_copy(1, b).start()
-
-        @pl.when(jnp.logical_not(is_inner))
-        def _():
-            g_copy(0, b).start()
-            x_wait(b)
+
+        @pl.when(is_inner)
+        def _():
+            g_copy(1, b, zr.at[b]).start()
+
+        if half > 1:
+            @pl.when(jnp.logical_not(is_inner))
+            def _():
+                @pl.when(b < passed)
+                def _():
+                    g_copy(0, b, ze.at[mine - 1, b]).start()
+
+                @pl.when(b >= passed)
+                def _():
+                    g_copy(1, b, zr.at[b]).start()
+                    g_copy(0, b, zr.at[b]).start()
+
+                x_wait(b)
 
         gw[...] += lax.dot_general(xg[rows(b), :], grad, (((0,), (0,)), ((), ())), preferred_element_type=F32)
 
     def gx_down(j, b):
         return remote(ge.at[j - 1, b], gx.at[rows(b), :], ges.at[j - 1], ger.at[0], {"feat": end_at(j)})
 
+    def turn_weight():
+        w_swap(False).wait_recv()
+        for j in range(half):
+            wt[:, pl.ds(j * width, width)] = wg[xcols(end_at(j)), :].T
+
     def finish(b):
         @pl.when(is_inner)
         def _():
-            @pl.when(b == 0)
-            def _():
-                w_swap(False).wait_recv()
-
             g_wait(b)
-
-            def grad_of(z):
-                return lax.dot_general(
-                    gg[rows(b), :], wg[xcols(z), :], (((1,), (1,)), ((), ())), preferred_element_type=F32
-                ).astype(BF)
-
+            grads = jnp.dot(gg[rows(b), :], wt[...], preferred_element_type=F32).astype(BF)
             for j in ends:
-                ge[j - 1, b] = grad_of(end_at(j))
+                ge[j - 1, b] = grads[:, j * width : (j + 1) * width]
                 gx_down(j, b).start()
-            gx[rows(b), :] = grad_of(me)
-
-    loop(make_grad)
+            gx[rows(b), :] = grads[:, :width]
+
+    def backward_step(c):
+        @pl.when(c + straight + 1 < blocks)
+        def _():
+            send_near(c + straight + 1)
+
+        make_grad(c, False)
+
+    for c in range(straight):
+        make_grad(c, True)
+        for ahead in ((straight, straight + 1) if c == 0 else (c + straight + 1,)):
+            if ahead < blocks:
+                send_near(ahead)
+    loop(straight, blocks, backward_step)
+
     gwb[...] = gw[...].astype(BF)
     height = gw.shape[0]
     for stage in range(stages):
@@ -424,7 +530,13 @@
             _, there, peer = stage_peer(stage, step)
             remote(src.at[part(there), :], buf.at[step - 1], rs_s.at[0], rs_r.at[0], {"blk": peer}).start()
         if stage == 0:
-            for b in range(blocks - 2):
+            @pl.when(is_inner)
+            def _():
+                for b in range(passed):
+                    g_pass(b)
+                turn_weight()
+
+            for b in range(straight):
                 finish(b)
         digit, _, _ = stage_peer(stage, 1)
         if stage == 0:
@@ -440,7 +552,7 @@
             piece = out.at[part(digit), :]
             remote(piece, piece, ag_s.at[0], ag_r.at[0], {"blk": peer}).start()
         if stage == 0:
-            for b in range(max(blocks - 2, 0), blocks):
+            for b in range(straight, blocks):
                 finish(b)
         piece = out.at[pl.ds(0, height - chunk), :]
         remote(piece, piece, ag_s.at[0], ag_r.at[0], owner_at(PAIR)).wait_recv()
@@ -456,11 +568,12 @@
     def sent_all(ref, sem):
         remote(ref, ref, sem, ger.at[0], owner_at(PAIR)).wait_send()
 
-    sent_all(gg.at[:, ocols(me)], zs.at[1])
-
     @pl.when(is_inner)
     def _():
         sent_all(x, xs.at[1])
+        sent_all(gg.at[:, ocols(me)], zs.at[1])
+        if half > 1:
+            sent_all(gg.at[pl.ds(0, passed * side), pl.ds(0, (half - 1) * ow)], zl.at[0])
         for j in ends:
             sent_all(pe.at[j - 1], es.at[j - 1])
             sent_all(ge.at[j - 1], ges.at[j - 1])
@@ -470,22 +583,33 @@
     def _():
         sent_all(x, xs.at[1])
         sent_all(x, xs.at[0])
+        sent_all(gg.at[pl.ds(0, (blocks - passed) * side), ocols(me)], zs.at[1])
         sent_all(gg.at[:, ocols(me)], zs.at[0])
         remote(gx, gx, ges.at[0], ger.at[0], {"feat": inner}).wait_recv()
 
-    for role in (PAIR, CROSS, AHEAD, BEHIND):
+    for role in (PAIR, CROSS):
         sent_all(hid[role], hs.at[role])
+    for role, count in ((OWN, wound), (offs, wound), (AHEAD, blocks - wound), (BEHIND, blocks - wound)):
+        if count:
+            sent_all(hid[OWN].at[pl.ds(0, count)], hs.at[role])
+    for role in (PAIR, CROSS):
         sent_all(sent.at[role], gs.at[role])
+    for role in (AHEAD, BEHIND):
+        sent_all(sent.at[role, pl.ds(0, straight)], gs.at[role])
+    if straight < blocks:
+        sent_all(sent.at[OWN, pl.ds(straight, blocks - straight)], gs.at[OWN])
+        sent_all(sent.at[OWN, pl.ds(straight, blocks - straight)], gs.at[offs])
 
     @pl.when(is_inner)
     def _():
         w_swap(True).wait_send()
-        for j in ends:
-            w_across(end_at(j)).wait_send()
+        for j in ends if group > 1 else ():
+            sent_all(w_rest(j), ws.at[j])
 
     @pl.when(jnp.logical_not(is_inner))
     def _():
-        w_up().wait_send()
+        if half > 1:
+            w_up().wait_send()
 
 
 def write_out(*refs):
@@ -540,16 +664,18 @@
             pltpu.VMEM((depth, ow), BF),
             pltpu.VMEM((spare, blocks, *block), BF),
             pltpu.VMEM((spare, blocks, side, width), BF),
+            pltpu.VMEM((nz * ow, nz // 2 * width), BF),
         ]
-        + [pltpu.VMEM((blocks, *block), BF)] * offs
+        + [pltpu.VMEM((blocks, *block), BF)] * 3
+        + [pltpu.VMEM((2, blocks, *block), BF)]
         + [pltpu.VMEM((f - 1, depth // f, ow), BF) for f in factors]
         + [pltpu.VMEM((depth, ow), BF) for f in factors]
         + [dma((2,)), dma((blocks,)), dma((spare,))]
-        + [dma((offs,)), dma((2, blocks)), dma((offs,))]
-        + [dma((offs,)), dma((2, blocks))]
-        + [dma((2,)), dma((blocks,))]
+        + [dma((offs + 1,)), dma((blocks,)), dma((2, blocks)), dma((offs,))]
+        + [dma((offs + 1,)), dma((3, blocks))]
+        + [dma((2,)), dma((blocks,)), dma((1,)), dma((spare, blocks))]
         + [dma((spare,)), dma((spare,)), dma((1,))]
-        + [dma((2, nz)), dma((nz, 2)), dma((1,)), dma((1,)), dma((7,))]
+        + [dma((spare + 1,)), dma((spare, 2)), dma((1,)), dma((1,)), dma((7,))]
         + psems,
         compiler_params=pltpu.CompilerParams(
             collective_id=0, has_side_effects=True, vmem_limit_bytes=32 * 1024 * 1024

time: 54.9 us -> 53.3 us (0.971)
  Pallas kernels: 54.1 us -> 52.5 us
    pallas_call x1, Pallas kernels: 53.2 us -> 51.6 us  [on_device(): pl.pallas_call(functools.partial(layer_kernel, dims), out_shape=(pltpu.VM...]
where the time goes in v4:
time: 53.3 us; the launch traced here: 53.1 us
  Pallas kernels  52.5 us (98%)
  between operations  0.64 us (1%)
    pallas_call x1, Pallas kernels, on_device(): pl.pallas_call(functools.partial(layer_kernel, dims), out_shape=(pltpu.VM...  51.6 us

profile of v4, /device:TPU:0, one launch (start us, length us, event | category | flops | bytes accessed | tf_op | source)
XLA Modules:
  0.0 53.1 jit_solution(13909069612128070079)
XLA Ops:
  0.6 51.6 %shard_map.94 = (bf16[1024,128]{1,0:T(8,128)(2,1)S(1)}, bf16[1024,128]{1,0:T(8,128)(2,1)S(1)}, f32[512,128]{1,0:T(8,128)S(1)}) custom-call(bf16[1024,128]{1,0:T(8,128)(2,1)} %x.1, bf16[512,128]{1,0:T(8,128)(2,1)} %w_in.1, bf16[1,5,8,128,128]{4,3,2,1,0:T(8,128)(2,1)} %tv_in.1, s32[5,1,8]{2,1,0:T(1,128)} %bitcast.2, s32[5,1,8]{2,1,0:T(1,128)} %bitcast.3, ...), custom_call_target="tpu_custom_call" | custom-call | tf_op jit(solution)/shard_map/pallas_call | solution.py:640
  52.2 0.9 %shard_map.95 = (bf16[1024,128]{1,0:T(8,128)(2,1)}, bf16[1024,128]{1,0:T(8,128)(2,1)}, f32[512,128]{1,0:T(8,128)}) custom-call(bf16[1024,128]{1,0:T(8,128)(2,1)S(1)} %get-tuple-element.6.refs_0_, bf16[1024,128]{1,0:T(8,128)(2,1)S(1)} %get-tuple-element.7.refs_1_, f32[512,128]{1,0:T(8,128)S(1)} %get-tuple-element.8.refs_2_), custom_call_target="tpu_custom_call" | custom-call | tf_op jit(solution)/shard_map/pallas_call | solution.py:684

commit v5 on v4

--- a/solution.py
+++ b/solution.py
@@ -33,7 +33,7 @@
 ):
     nb, nz, offs, slots, blocks, side, width, ow, factors = dims
     stages = len(factors)
-    hid, hid_far, rest = rest[:3], rest[3], rest[4:]
+    hid, hid_two, rest = rest[:3], rest[3:5], rest[5:]
     gathered, summed = rest[:stages], rest[stages : 2 * stages]
     (xs, xr, xb, hs, hr, hf, hall, gs, gr, zs, zr, zl, ze, es, ges, ger, ws, wr, ks, kr, near) = rest[2 * stages : 2 * stages + 21]
     psems = rest[2 * stages + 21 :]
@@ -52,8 +52,8 @@
     ends = range(1, half)
     mine = jnp.where(lower, half - 1 - me, me - half)
     straight = min(3, blocks)
-    passed = blocks // 2
-    wound = blocks // 2
+    wound = min(blocks // 2 + 1, blocks)
+    passing = range(straight, max(blocks - 2, straight))
 
     def end_at(j):
         return jnp.where(lower, half - 1 - j, half + j)
@@ -184,51 +184,49 @@
     for copy in local[:3]:
         copy.wait()
 
-    near_slot = jnp.where(ahead_near, 0, 1)
-    far_slot = 1 - near_slot
+    def by_side(run):
+        pl.when(ahead_near)(functools.partial(run, 0))
+        pl.when(jnp.logical_not(ahead_near))(functools.partial(run, 1))
 
     def hid_pair(b):
         return remote(hid[OWN].at[b], hid[PAIR].at[b], hs.at[PAIR], hall.at[PAIR], owner_at(PAIR))
 
     def hid_straight(role, b):
         slot = int(role == AHEAD)
-        return remote(hid[OWN].at[b], hid_far.at[slot, b], hs.at[role], hf.at[slot, b], owner_at(role))
-
-    def hid_near(b):
-        return remote(hid[OWN].at[b], hid_far.at[far_slot, b], hs.at[OWN], hf.at[far_slot, b], near_owner)
-
-    def hid_side(b):
-        return remote(
-            hid_far.at[near_slot, b], hid_far.at[far_slot, b], hs.at[offs], hf.at[far_slot, b], side_source
-        )
+        return remote(hid[OWN].at[b], hid_two[slot].at[b], hs.at[role], hf.at[slot, b], owner_at(role))
+
+    def hid_near(near, b):
+        return remote(hid[OWN].at[b], hid_two[1 - near].at[b], hs.at[OWN], hf.at[1 - near, b], near_owner)
+
+    def hid_side(near, b):
+        return remote(hid_two[near].at[b], hid_two[1 - near].at[b], hs.at[offs], hf.at[1 - near, b], side_source)
 
     def hid_passed(b):
-        return remote(hid_far.at[0, b], hid[CROSS].at[b], hs.at[CROSS], hall.at[CROSS], owner_at(PAIR))
+        return remote(hid_two[0].at[b], hid[CROSS].at[b], hs.at[CROSS], hall.at[CROSS], owner_at(PAIR))
 
     def hid_landed(slot, b):
-        piece = hid_far.at[slot, b]
+        piece = hid_two[slot].at[b]
         remote(piece, piece, hs.at[OWN], hf.at[slot, b], owner_at(PAIR)).wait_recv()
 
     def hid_whole(role):
         remote(hid[role], hid[role], hs.at[role], hall.at[role], owner_at(PAIR)).wait_recv()
 
     def take_near(b):
-        hid_landed(near_slot, b)
-
-        @pl.when(b < wound)
-        def _():
-            hid_side(b).start()
-
-        @pl.when(ahead_near)
-        def _():
-            hid_passed(b).start()
+        def run(near):
+            hid_landed(near, b)
+            hid_side(near, b).start()
+            if near == 0:
+                hid_passed(b).start()
+
+        by_side(run)
 
     def take_far(b):
-        hid_landed(far_slot, b)
-
-        @pl.when(jnp.logical_not(ahead_near))
-        def _():
-            hid_passed(b).start()
+        def run(near):
+            hid_landed(1 - near, b)
+            if near == 1:
+                hid_passed(b).start()
+
+        by_side(run)
 
     def hid_down(j, b):
         return remote(pe.at[j - 1, b], hid[OWN].at[b], es.at[j - 1], hr.at[b], {"feat": end_at(j)})
@@ -238,7 +236,7 @@
 
         @pl.when(b < wound)
         def _():
-            hid_near(b).start()
+            by_side(lambda near: hid_near(near, b).start())
 
         @pl.when(b >= wound)
         def _():
@@ -253,7 +251,7 @@
             pe[j - 1, b] = hidden_of(end_at(j), b)
             hid_down(j, b).start()
 
-    lag = min(3, blocks)
+    lag = min(4, blocks)
     first = min(2, blocks - 1)
 
     def forward_step(b, carry):
@@ -324,7 +322,7 @@
         k = offset_of(role)
         for s in range(slots):
             c = tc[k, 0, s]
-            source = hid[role][c] if role < AHEAD else hid_far[role - AHEAD, c]
+            source = (hid[role] if role < AHEAD else hid_two[role - AHEAD])[c]
             prod[role, s] = jnp.dot(tv[k, s], source, preferred_element_type=F32)
 
     def weight_of(table, k, s, b):
@@ -346,14 +344,18 @@
         lax.fori_loop(0, blocks, add, 0)
 
     gather_role(OWN)
+    for b in range(blocks - lag, wound):
+        take_near(b)
     hid_whole(PAIR)
     gather_role(PAIR)
-    for b in range(max(blocks - lag, 0), blocks):
-        take_near(b)
-    for b in range(blocks):
+    for b in range(wound):
         take_far(b)
-
+    for b in range(wound, blocks):
+        hid_landed(0, b)
+        hid_passed(b).start()
     gather_role(AHEAD)
+    for b in range(wound, blocks):
+        hid_landed(1, b)
     gather_role(BEHIND)
     local[3].wait()
     hid_whole(CROSS)
@@ -402,15 +404,26 @@
         sent[AHEAD, c] = column_sum(AHEAD, offset_of(AHEAD), c, start).astype(BF)
         sum_copy(AHEAD, c).start()
 
+    def side_copy(c):
+        return remote(sent.at[far_role, c], got.at[OWN, c], gs.at[OWN], gr.at[2, c], side_owner)
+
+    def send_side_early(c):
+        sent[BEHIND, c] = column_sum(BEHIND, offset_of(BEHIND), c, None).astype(BF)
+        side_copy(c).start()
+
+    def send_side_late(c):
+        cross_wait(c)
+        start = got[CROSS, c].astype(F32)
+        sent[AHEAD, c] = column_sum(AHEAD, offset_of(AHEAD), c, start).astype(BF)
+        side_copy(c).start()
+
     crossing_near = jnp.where(ahead_near, 1.0, 0.0).astype(F32)
 
-    def send_side(c):
-        cross_wait(c)
-        start = got[CROSS, c].astype(F32) * (1.0 - crossing_near)
-        sent[far_role, c] = column_sum(far_role, reach - near_lean, c, start).astype(BF)
-        remote(sent.at[far_role, c], got.at[OWN, c], gs.at[OWN], gr.at[2, c], side_owner).start()
-
     def send_near(c):
+        @pl.when(ahead_near)
+        def _():
+            cross_wait(c)
+
         start = got[CROSS, c].astype(F32) * crossing_near
         total = column_sum(near_role, reach + near_lean, c, start)
         piece = got.at[OWN, c]
@@ -428,12 +441,24 @@
     backward_products(CROSS)
     loop(0, blocks, lambda c: send_sum(CROSS, c))
     backward_products(BEHIND)
-    for c in range(straight):
+    send_sum(BEHIND, 0)
+
+    @pl.when(ahead_near)
+    def _():
+        for c in range(straight, blocks):
+            send_side_early(c)
+
+    backward_products(AHEAD)
+    send_joint(0)
+
+    @pl.when(jnp.logical_not(ahead_near))
+    def _():
+        for c in range(straight, blocks):
+            send_side_late(c)
+
+    for c in range(1, straight):
         send_sum(BEHIND, c)
-    backward_products(AHEAD)
-    for c in range(straight):
         send_joint(c)
-    loop(straight, blocks, send_side)
     backward_products(PAIR)
     loop(0, blocks, lambda c: send_sum(PAIR, c))
     backward_products(OWN)
@@ -445,7 +470,7 @@
         return remote(piece, piece, zs.at[way], landed, {"feat": (inner, other)[way]})
 
     def g_wait(b):
-        piece = gg.at[rows(b), pl.ds(0, (half if b < passed else nz - 1) * ow)]
+        piece = gg.at[rows(b), pl.ds(0, (half if b in passing else nz - 1) * ow)]
         remote(piece, piece, zs.at[0], zr.at[b], {"feat": other}).wait_recv()
 
     def g_pass(b):
@@ -453,6 +478,12 @@
             piece = gg.at[rows(b), ocols(end_at(j))]
             remote(piece, piece, zl.at[0], ze.at[j - 1, b], {"feat": other}).wait_recv()
             remote(piece, piece, zl.at[0], zr.at[b], {"feat": other}).start()
+
+    def pass_on(some):
+        @pl.when(is_inner)
+        def _():
+            for b in some:
+                g_pass(b)
 
     def make_grad(b, two):
         pieces = got.at[pl.ds(0, 3 if two else 2), b]
@@ -470,11 +501,13 @@
         if half > 1:
             @pl.when(jnp.logical_not(is_inner))
             def _():
-                @pl.when(b < passed)
+                passes = (b >= passing.start) & (b < passing.stop)
+
+                @pl.when(passes)
                 def _():
                     g_copy(0, b, ze.at[mine - 1, b]).start()
 
-                @pl.when(b >= passed)
+                @pl.when(jnp.logical_not(passes))
                 def _():
                     g_copy(1, b, zr.at[b]).start()
                     g_copy(0, b, zr.at[b]).start()
@@ -501,19 +534,15 @@
                 gx_down(j, b).start()
             gx[rows(b), :] = grads[:, :width]
 
-    def backward_step(c):
-        @pl.when(c + straight + 1 < blocks)
-        def _():
-            send_near(c + straight + 1)
-
-        make_grad(c, False)
-
-    for c in range(straight):
-        make_grad(c, True)
-        for ahead in ((straight, straight + 1) if c == 0 else (c + straight + 1,)):
-            if ahead < blocks:
-                send_near(ahead)
-    loop(straight, blocks, backward_step)
+    @pl.when(is_inner)
+    def _():
+        turn_weight()
+
+    waiting = list(range(straight, blocks))
+    for c in range(blocks):
+        for later in waiting[c : c + 1]:
+            send_near(later)
+        make_grad(c, c < straight)
 
     gwb[...] = gw[...].astype(BF)
     height = gw.shape[0]
@@ -530,14 +559,9 @@
             _, there, peer = stage_peer(stage, step)
             remote(src.at[part(there), :], buf.at[step - 1], rs_s.at[0], rs_r.at[0], {"blk": peer}).start()
         if stage == 0:
-            @pl.when(is_inner)
-            def _():
-                for b in range(passed):
-                    g_pass(b)
-                turn_weight()
-
             for b in range(straight):
                 finish(b)
+            pass_on(passing)
         digit, _, _ = stage_peer(stage, 1)
         if stage == 0:
             total = gw[part(digit), :]
@@ -552,7 +576,12 @@
             piece = out.at[part(digit), :]
             remote(piece, piece, ag_s.at[0], ag_r.at[0], {"blk": peer}).start()
         if stage == 0:
-            for b in range(straight, blocks):
+            late = list(range(passing.stop, blocks))
+            for b in passing:
+                finish(b)
+                if late:
+                    finish(late.pop(0))
+            for b in late:
                 finish(b)
         piece = out.at[pl.ds(0, height - chunk), :]
         remote(piece, piece, ag_s.at[0], ag_r.at[0], owner_at(PAIR)).wait_recv()
@@ -572,8 +601,8 @@
     def _():
         sent_all(x, xs.at[1])
         sent_all(gg.at[:, ocols(me)], zs.at[1])
-        if half > 1:
-            sent_all(gg.at[pl.ds(0, passed * side), pl.ds(0, (half - 1) * ow)], zl.at[0])
+        if half > 1 and passing:
+            sent_all(gg.at[pl.ds(0, len(passing) * side), pl.ds(0, (half - 1) * ow)], zl.at[0])
         for j in ends:
             sent_all(pe.at[j - 1], es.at[j - 1])
             sent_all(ge.at[j - 1], ges.at[j - 1])
@@ -583,7 +612,7 @@
     def _():
         sent_all(x, xs.at[1])
         sent_all(x, xs.at[0])
-        sent_all(gg.at[pl.ds(0, (blocks - passed) * side), ocols(me)], zs.at[1])
+        sent_all(gg.at[pl.ds(0, (blocks - len(passing)) * side), ocols(me)], zs.at[1])
         sent_all(gg.at[:, ocols(me)], zs.at[0])
         remote(gx, gx, ges.at[0], ger.at[0], {"feat": inner}).wait_recv()
 
@@ -666,8 +695,7 @@
             pltpu.VMEM((spare, blocks, side, width), BF),
             pltpu.VMEM((nz * ow, nz // 2 * width), BF),
         ]
-        + [pltpu.VMEM((blocks, *block), BF)] * 3
-        + [pltpu.VMEM((2, blocks, *block), BF)]
+        + [pltpu.VMEM((blocks, *block), BF)] * 5
         + [pltpu.VMEM((f - 1, depth // f, ow), BF) for f in factors]
         + [pltpu.VMEM((depth, ow), BF) for f in factors]
         + [dma((2,)), dma((blocks,)), dma((spare,))]

time: 53.3 us -> 51.9 us (0.974)
  Pallas kernels: 52.5 us -> 51.1 us
    pallas_call x1, Pallas kernels: 51.6 us -> 50.2 us  [on_device(): pl.pallas_call(functools.partial(layer_kernel, dims), out_shape=(pltpu.VM...]
where the time goes in v5:
time: 51.9 us; the launch traced here: 51.7 us
  Pallas kernels  51.1 us (98%)
  between operations  0.64 us (1%)
    pallas_call x1, Pallas kernels, on_device(): pl.pallas_call(functools.partial(layer_kernel, dims), out_shape=(pltpu.VM...  50.2 us

profile of v5, /device:TPU:0, one launch (start us, length us, event | category | flops | bytes accessed | tf_op | source)
XLA Modules:
  0.0 51.7 jit_solution(347230602352598958)
XLA Ops:
  0.6 50.2 %shard_map.94 = (bf16[1024,128]{1,0:T(8,128)(2,1)S(1)}, bf16[1024,128]{1,0:T(8,128)(2,1)S(1)}, f32[512,128]{1,0:T(8,128)S(1)}) custom-call(bf16[1024,128]{1,0:T(8,128)(2,1)} %x.1, bf16[512,128]{1,0:T(8,128)(2,1)} %w_in.1, bf16[1,5,8,128,128]{4,3,2,1,0:T(8,128)(2,1)} %tv_in.1, s32[5,1,8]{2,1,0:T(1,128)} %bitcast.2, s32[5,1,8]{2,1,0:T(1,128)} %bitcast.3, ...), custom_call_target="tpu_custom_call" | custom-call | tf_op jit(solution)/shard_map/pallas_call | solution.py:669
  50.8 0.9 %shard_map.95 = (bf16[1024,128]{1,0:T(8,128)(2,1)}, bf16[1024,128]{1,0:T(8,128)(2,1)}, f32[512,128]{1,0:T(8,128)}) custom-call(bf16[1024,128]{1,0:T(8,128)(2,1)S(1)} %get-tuple-element.6.refs_0_, bf16[1024,128]{1,0:T(8,128)(2,1)S(1)} %get-tuple-element.7.refs_1_, f32[512,128]{1,0:T(8,128)S(1)} %get-tuple-element.8.refs_2_), custom_call_target="tpu_custom_call" | custom-call | tf_op jit(solution)/shard_map/pallas_call | solution.py:712

commit v6 on v5

--- a/solution.py
+++ b/solution.py
@@ -35,8 +35,8 @@
     stages = len(factors)
     hid, hid_two, rest = rest[:3], rest[3:5], rest[5:]
     gathered, summed = rest[:stages], rest[stages : 2 * stages]
-    (xs, xr, xb, hs, hr, hf, hall, gs, gr, zs, zr, zl, ze, es, ges, ger, ws, wr, ks, kr, near) = rest[2 * stages : 2 * stages + 21]
-    psems = rest[2 * stages + 21 :]
+    (xs, xr, xb, hs, hr, hf, hall, gs, gr, gy, zs, zr, zl, ze, es, ges, ger, ws, wr, ks, kr, near) = rest[2 * stages : 2 * stages + 22]
+    psems = rest[2 * stages + 22 :]
     reach = (offs - 1) // 2
     half = nz // 2
     me = lax.axis_index("feat")
@@ -53,7 +53,8 @@
     mine = jnp.where(lower, half - 1 - me, me - half)
     straight = min(3, blocks)
     wound = min(blocks // 2 + 1, blocks)
-    passing = range(straight, max(blocks - 2, straight))
+    passing = range(min(2, blocks), max(blocks - 2, 2))
+    last = blocks - 1
 
     def end_at(j):
         return jnp.where(lower, half - 1 - j, half + j)
@@ -134,6 +135,10 @@
             x.at[rows(b), :], xg.at[rows(b), xcols(me)], xs.at[way], xr.at[b], {"feat": (inner, other)[way]}
         )
 
+    def x_own(j, b):
+        piece = xg.at[rows(b), xcols(me)]
+        return remote(x.at[rows(b), :], piece, xb.at[j - 1], xr.at[b], {"feat": end_at(j)})
+
     def x_back(s, e, j, b):
         piece = xg.at[rows(b), xcols(s)]
         return remote(piece, piece, xb.at[j - 1], xr.at[b], {"feat": e})
@@ -172,6 +177,8 @@
     def _():
         for b in range(min(6, blocks)):
             x_copy(1, b).start()
+            for j in ends:
+                x_own(j, b).start()
 
     @pl.when(jnp.logical_not(is_inner))
     def _():
@@ -189,27 +196,27 @@
         pl.when(jnp.logical_not(ahead_near))(functools.partial(run, 1))
 
     def hid_pair(b):
-        return remote(hid[OWN].at[b], hid[PAIR].at[b], hs.at[PAIR], hall.at[PAIR], owner_at(PAIR))
+        return remote(hid[OWN].at[b], hid[PAIR].at[b], hs.at[0], hall.at[0], owner_at(PAIR))
 
     def hid_straight(role, b):
         slot = int(role == AHEAD)
-        return remote(hid[OWN].at[b], hid_two[slot].at[b], hs.at[role], hf.at[slot, b], owner_at(role))
+        return remote(hid[OWN].at[b], hid_two[slot].at[b], hs.at[0], hf.at[slot, b], owner_at(role))
 
     def hid_near(near, b):
-        return remote(hid[OWN].at[b], hid_two[1 - near].at[b], hs.at[OWN], hf.at[1 - near, b], near_owner)
+        return remote(hid[OWN].at[b], hid_two[1 - near].at[b], hs.at[0], hf.at[1 - near, b], near_owner)
 
     def hid_side(near, b):
-        return remote(hid_two[near].at[b], hid_two[1 - near].at[b], hs.at[offs], hf.at[1 - near, b], side_source)
+        return remote(hid_two[near].at[b], hid_two[1 - near].at[b], hs.at[0], hf.at[1 - near, b], side_source)
 
     def hid_passed(b):
-        return remote(hid_two[0].at[b], hid[CROSS].at[b], hs.at[CROSS], hall.at[CROSS], owner_at(PAIR))
+        return remote(hid_two[0].at[b], hid[CROSS].at[b], hs.at[0], hall.at[1], owner_at(PAIR))
 
     def hid_landed(slot, b):
         piece = hid_two[slot].at[b]
-        remote(piece, piece, hs.at[OWN], hf.at[slot, b], owner_at(PAIR)).wait_recv()
+        remote(piece, piece, hs.at[0], hf.at[slot, b], owner_at(PAIR)).wait_recv()
 
     def hid_whole(role):
-        remote(hid[role], hid[role], hs.at[role], hall.at[role], owner_at(PAIR)).wait_recv()
+        remote(hid[role], hid[role], hs.at[0], hall.at[int(role == CROSS)], owner_at(PAIR)).wait_recv()
 
     def take_near(b):
         def run(near):
@@ -260,6 +267,8 @@
             @pl.when(b + 6 < blocks)
             def _():
                 x_copy(1, b + 6).start()
+                for j in ends:
+                    x_own(j, b + 6).start()
 
         per_block = slots // blocks
         for role in range(offs):
@@ -308,7 +317,7 @@
         w_swap(True).start()
         for j in ends:
             for b in range(blocks):
-                for step in range(nz):
+                for step in range(1, nz):
                     s = lax.rem(me + step, nz)
 
                     @pl.when(s != end_at(j))
@@ -387,12 +396,12 @@
 
     def sum_copy(role, c):
         return remote(
-            sent.at[role, c], got.at[arrives[role], c], gs.at[role], gr.at[int(role == CROSS), c], owner_at(target[role])
+            sent.at[role, c], got.at[arrives[role], c], gs.at[0], gr.at[int(role == CROSS), c], owner_at(target[role])
         )
 
     def cross_wait(c):
         piece = got.at[CROSS, c]
-        remote(piece, piece, gs.at[CROSS], gr.at[1, c], owner_at(PAIR)).wait_recv()
+        remote(piece, piece, gs.at[0], gr.at[1, c], owner_at(PAIR)).wait_recv()
 
     def send_sum(role, c):
         sent[role, c] = column_sum(role, offset_of(role), c, None).astype(BF)
@@ -405,7 +414,7 @@
         sum_copy(AHEAD, c).start()
 
     def side_copy(c):
-        return remote(sent.at[far_role, c], got.at[OWN, c], gs.at[OWN], gr.at[2, c], side_owner)
+        return remote(sent.at[far_role, c], got.at[OWN, c], gs.at[0], gy.at[c - straight], side_owner)
 
     def send_side_early(c):
         sent[BEHIND, c] = column_sum(BEHIND, offset_of(BEHIND), c, None).astype(BF)
@@ -427,9 +436,9 @@
         start = got[CROSS, c].astype(F32) * crossing_near
         total = column_sum(near_role, reach + near_lean, c, start)
         piece = got.at[OWN, c]
-        remote(piece, piece, gs.at[OWN], gr.at[2, c], side_owner).wait_recv()
+        remote(piece, piece, gs.at[0], gy.at[c - straight], side_owner).wait_recv()
         sent[near_role, c] = (total + got[OWN, c].astype(F32)).astype(BF)
-        remote(sent.at[near_role, c], got.at[AHEAD, c], gs.at[offs], gr.at[0, c], near_owner).start()
+        remote(sent.at[near_role, c], got.at[AHEAD, c], gs.at[0], gr.at[0, c], near_owner).start()
 
     def loop(low, high, step):
         def body(c, carry):
@@ -476,7 +485,7 @@
     def g_pass(b):
         for j in ends:
             piece = gg.at[rows(b), ocols(end_at(j))]
-            remote(piece, piece, zl.at[0], ze.at[j - 1, b], {"feat": other}).wait_recv()
+            remote(piece, piece, zl.at[0], ze.at[j - 1, b - passing.start], {"feat": other}).wait_recv()
             remote(piece, piece, zl.at[0], zr.at[b], {"feat": other}).start()
 
     def pass_on(some):
@@ -488,7 +497,7 @@
     def make_grad(b, two):
         pieces = got.at[pl.ds(0, 3 if two else 2), b]
         total = column_sum(OWN, reach, b, gp[b].astype(F32))
-        remote(pieces, pieces, gs.at[PAIR], gr.at[0, b], owner_at(PAIR)).wait_recv()
+        remote(pieces, pieces, gs.at[0], gr.at[0, b], owner_at(PAIR)).wait_recv()
         for role in (PAIR, AHEAD, BEHIND)[: 3 if two else 2]:
             total = total + got[role, b].astype(F32)
         grad = total.astype(BF)
@@ -505,7 +514,7 @@
 
                 @pl.when(passes)
                 def _():
-                    g_copy(0, b, ze.at[mine - 1, b]).start()
+                    g_copy(0, b, ze.at[mine - 1, b - passing.start]).start()
 
                 @pl.when(jnp.logical_not(passes))
                 def _():
@@ -555,11 +564,16 @@
         def part(q):
             return pl.ds(pl.multiple_of(q * chunk, chunk), chunk)
 
-        for step in range(1, size):
+        steps = range(1, size)
+        if stage == 0 and size % 4 == 0 and size >= 8:
+            near_step = 2 * (1 - 2 * lax.rem(chip, 2))
+            hops = [-near_step, near_step] + [2 * h for h in range(2, size // 2 - 1)]
+            steps = [lax.rem(h + t + size, size) for h in hops for t in (0, turn)] + [lax.rem(turn + size, size)]
+        for step in steps:
             _, there, peer = stage_peer(stage, step)
             remote(src.at[part(there), :], buf.at[step - 1], rs_s.at[0], rs_r.at[0], {"blk": peer}).start()
         if stage == 0:
-            for b in range(straight):
+            for b in range(passing.start):
                 finish(b)
             pass_on(passing)
         digit, _, _ = stage_peer(stage, 1)
@@ -571,7 +585,7 @@
         for step in range(1, size):
             total = total + buf[step - 1].astype(F32)
         out[part(digit), :] = total.astype(BF)
-        for step in range(1, size):
+        for step in steps:
             _, _, peer = stage_peer(stage, step)
             piece = out.at[part(digit), :]
             remote(piece, piece, ag_s.at[0], ag_r.at[0], {"blk": peer}).start()
@@ -579,7 +593,7 @@
             late = list(range(passing.stop, blocks))
             for b in passing:
                 finish(b)
-                if late:
+                if b != passing.start and late:
                     finish(late.pop(0))
             for b in late:
                 finish(b)
@@ -616,18 +630,8 @@
         sent_all(gg.at[:, ocols(me)], zs.at[0])
         remote(gx, gx, ges.at[0], ger.at[0], {"feat": inner}).wait_recv()
 
-    for role in (PAIR, CROSS):
-        sent_all(hid[role], hs.at[role])
-    for role, count in ((OWN, wound), (offs, wound), (AHEAD, blocks - wound), (BEHIND, blocks - wound)):
-        if count:
-            sent_all(hid[OWN].at[pl.ds(0, count)], hs.at[role])
-    for role in (PAIR, CROSS):
-        sent_all(sent.at[role], gs.at[role])
-    for role in (AHEAD, BEHIND):
-        sent_all(sent.at[role, pl.ds(0, straight)], gs.at[role])
-    if straight < blocks:
-        sent_all(sent.at[OWN, pl.ds(straight, blocks - straight)], gs.at[OWN])
-        sent_all(sent.at[OWN, pl.ds(straight, blocks - straight)], gs.at[offs])
+    sent_all(got.at[pl.ds(0, 4)], hs.at[0])
+    sent_all(got.at[pl.ds(0, 4)], gs.at[0])
 
     @pl.when(is_inner)
     def _():
@@ -699,9 +703,9 @@
         + [pltpu.VMEM((f - 1, depth // f, ow), BF) for f in factors]
         + [pltpu.VMEM((depth, ow), BF) for f in factors]
         + [dma((2,)), dma((blocks,)), dma((spare,))]
-        + [dma((offs + 1,)), dma((blocks,)), dma((2, blocks)), dma((offs,))]
-        + [dma((offs + 1,)), dma((3, blocks))]
-        + [dma((2,)), dma((blocks,)), dma((1,)), dma((spare, blocks))]
+        + [dma((1,)), dma((blocks,)), dma((2, blocks)), dma((2,))]
+        + [dma((1,)), dma((2, blocks)), dma((max(blocks - 3, 1),))]
+        + [dma((2,)), dma((blocks,)), dma((1,)), dma((spare, max(blocks - 4, 1)))]
         + [dma((spare,)), dma((spare,)), dma((1,))]
         + [dma((spare + 1,)), dma((spare, 2)), dma((1,)), dma((1,)), dma((7,))]
         + psems,

time: 51.9 us -> 51.9 us (level)
  no operation moved by 1% of the time
where the time goes in v6:
time: 51.9 us; the launch traced here: 51.7 us
  Pallas kernels  51.1 us (98%)
  between operations  0.64 us (1%)
    pallas_call x1, Pallas kernels, on_device(): pl.pallas_call(functools.partial(layer_kernel, dims), out_shape=(pltpu.VM...  50.2 us

profile of v6, /device:TPU:0, one launch (start us, length us, event | category | flops | bytes accessed | tf_op | source)
XLA Modules:
  0.0 51.7 jit_solution(15823354572882185815)
XLA Ops:
  0.6 50.2 %shard_map.94 = (bf16[1024,128]{1,0:T(8,128)(2,1)S(1)}, bf16[1024,128]{1,0:T(8,128)(2,1)S(1)}, f32[512,128]{1,0:T(8,128)S(1)}) custom-call(bf16[1024,128]{1,0:T(8,128)(2,1)} %x.1, bf16[512,128]{1,0:T(8,128)(2,1)} %w_in.1, bf16[1,5,8,128,128]{4,3,2,1,0:T(8,128)(2,1)} %tv_in.1, s32[5,1,8]{2,1,0:T(1,128)} %bitcast.2, s32[5,1,8]{2,1,0:T(1,128)} %bitcast.3, ...), custom_call_target="tpu_custom_call" | custom-call | tf_op jit(solution)/shard_map/pallas_call | solution.py:673
  50.8 0.9 %shard_map.95 = (bf16[1024,128]{1,0:T(8,128)(2,1)}, bf16[1024,128]{1,0:T(8,128)(2,1)}, f32[512,128]{1,0:T(8,128)}) custom-call(bf16[1024,128]{1,0:T(8,128)(2,1)S(1)} %get-tuple-element.6.refs_0_, bf16[1024,128]{1,0:T(8,128)(2,1)S(1)} %get-tuple-element.7.refs_1_, f32[512,128]{1,0:T(8,128)S(1)} %get-tuple-element.8.refs_2_), custom_call_target="tpu_custom_call" | custom-call | tf_op jit(solution)/shard_map/pallas_call | solution.py:716

commit v7 on v6

--- a/solution.py
+++ b/solution.py
@@ -51,8 +51,8 @@
     is_inner = me == inner
     ends = range(1, half)
     mine = jnp.where(lower, half - 1 - me, me - half)
-    straight = min(3, blocks)
-    wound = min(blocks // 2 + 1, blocks)
+    straight = min(2, blocks)
+    wound = min(blocks // 2, blocks)
     passing = range(min(2, blocks), max(blocks - 2, 2))
     last = blocks - 1
 
@@ -248,6 +248,9 @@
         @pl.when(b >= wound)
         def _():
             hid_straight(AHEAD, b).start()
+
+        @pl.when(b >= wound)
+        def _():
             hid_straight(BEHIND, b).start()
 
     def hidden_of(z, b):
@@ -352,9 +355,9 @@
 
         lax.fori_loop(0, blocks, add, 0)
 
-    gather_role(OWN)
     for b in range(blocks - lag, wound):
         take_near(b)
+    gather_role(OWN)
     hid_whole(PAIR)
     gather_role(PAIR)
     for b in range(wound):
@@ -704,7 +707,7 @@
         + [pltpu.VMEM((depth, ow), BF) for f in factors]
         + [dma((2,)), dma((blocks,)), dma((spare,))]
         + [dma((1,)), dma((blocks,)), dma((2, blocks)), dma((2,))]
-        + [dma((1,)), dma((2, blocks)), dma((max(blocks - 3, 1),))]
+        + [dma((1,)), dma((2, blocks)), dma((blocks,))]
         + [dma((2,)), dma((blocks,)), dma((1,)), dma((spare, max(blocks - 4, 1)))]
         + [dma((spare,)), dma((spare,)), dma((1,))]
         + [dma((spare + 1,)), dma((spare, 2)), dma((1,)), dma((1,)), dma((7,))]

time: 51.9 us -> 51.5 us (level)
  no operation moved by 1% of the time
where the time goes in v7:
time: 51.5 us; the launch traced here: 51.4 us
  Pallas kernels  50.7 us (98%)
  between operations  0.64 us (1%)
    pallas_call x1, Pallas kernels, on_device(): pl.pallas_call(functools.partial(layer_kernel, dims), out_shape=(pltpu.VM...  49.8 us

profile of v7, /device:TPU:0, one launch (start us, length us, event | category | flops | bytes accessed | tf_op | source)
XLA Modules:
  0.0 51.4 jit_solution(11812813729752343966)
XLA Ops:
  0.6 49.8 %shard_map.94 = (bf16[1024,128]{1,0:T(8,128)(2,1)S(1)}, bf16[1024,128]{1,0:T(8,128)(2,1)S(1)}, f32[512,128]{1,0:T(8,128)S(1)}) custom-call(bf16[1024,128]{1,0:T(8,128)(2,1)} %x.1, bf16[512,128]{1,0:T(8,128)(2,1)} %w_in.1, bf16[1,5,8,128,128]{4,3,2,1,0:T(8,128)(2,1)} %tv_in.1, s32[5,1,8]{2,1,0:T(1,128)} %bitcast.2, s32[5,1,8]{2,1,0:T(1,128)} %bitcast.3, ...), custom_call_target="tpu_custom_call" | custom-call | tf_op jit(solution)/shard_map/pallas_call | solution.py:676
  50.5 0.9 %shard_map.95 = (bf16[1024,128]{1,0:T(8,128)(2,1)}, bf16[1024,128]{1,0:T(8,128)(2,1)}, f32[512,128]{1,0:T(8,128)}) custom-call(bf16[1024,128]{1,0:T(8,128)(2,1)S(1)} %get-tuple-element.6.refs_0_, bf16[1024,128]{1,0:T(8,128)(2,1)S(1)} %get-tuple-element.7.refs_1_, f32[512,128]{1,0:T(8,128)S(1)} %get-tuple-element.8.refs_2_), custom_call_target="tpu_custom_call" | custom-call | tf_op jit(solution)/shard_map/pallas_call | solution.py:719

commit v8 on v7

--- a/solution.py
+++ b/solution.py
@@ -35,8 +35,8 @@
     stages = len(factors)
     hid, hid_two, rest = rest[:3], rest[3:5], rest[5:]
     gathered, summed = rest[:stages], rest[stages : 2 * stages]
-    (xs, xr, xb, hs, hr, hf, hall, gs, gr, gy, zs, zr, zl, ze, es, ges, ger, ws, wr, ks, kr, near) = rest[2 * stages : 2 * stages + 22]
-    psems = rest[2 * stages + 22 :]
+    (xs, xr, xb, hs, hf, hall, gs, gr, gy, zs, zr, zl, ze, es, ges, ger, ws, wr, ks, kr, near) = rest[2 * stages : 2 * stages + 21]
+    psems = rest[2 * stages + 21 :]
     reach = (offs - 1) // 2
     half = nz // 2
     me = lax.axis_index("feat")
@@ -236,7 +236,7 @@
         by_side(run)
 
     def hid_down(j, b):
-        return remote(pe.at[j - 1, b], hid[OWN].at[b], es.at[j - 1], hr.at[b], {"feat": end_at(j)})
+        return remote(pe.at[j - 1, b], hid[OWN].at[b], es.at[j - 1], ze.at[0, b], {"feat": end_at(j)})
 
     def spread(b):
         hid_pair(b).start()
@@ -299,7 +299,7 @@
 
         @pl.when(jnp.logical_not(is_inner))
         def _():
-            remote(hid[OWN].at[b], hid[OWN].at[b], es.at[0], hr.at[b], {"feat": inner}).wait_recv()
+            remote(hid[OWN].at[b], hid[OWN].at[b], es.at[0], ze.at[0, b], {"feat": inner}).wait_recv()
             spread(b)
 
         @pl.when(b >= lag)
@@ -706,9 +706,9 @@
         + [pltpu.VMEM((f - 1, depth // f, ow), BF) for f in factors]
         + [pltpu.VMEM((depth, ow), BF) for f in factors]
         + [dma((2,)), dma((blocks,)), dma((spare,))]
-        + [dma((1,)), dma((blocks,)), dma((2, blocks)), dma((2,))]
-        + [dma((1,)), dma((2, blocks)), dma((blocks,))]
-        + [dma((2,)), dma((blocks,)), dma((1,)), dma((spare, max(blocks - 4, 1)))]
+        + [dma((1,)), dma((2, blocks)), dma((2,))]
+        + [dma((1,)), dma((2, blocks)), dma((max(blocks - 2, 1),))]
+        + [dma((2,)), dma((blocks,)), dma((1,)), dma((spare, blocks))]
         + [dma((spare,)), dma((spare,)), dma((1,))]
         + [dma((spare + 1,)), dma((spare, 2)), dma((1,)), dma((1,)), dma((7,))]
         + psems,

time: 51.5 us -> 51.5 us (level)
  no operation moved by 1% of the time
where the time goes in v8:
time: 51.5 us; the launch traced here: 51.3 us
  Pallas kernels  50.7 us (98%)
  between operations  0.64 us (1%)
    pallas_call x1, Pallas kernels, on_device(): pl.pallas_call(functools.partial(layer_kernel, dims), out_shape=(pltpu.VM...  49.8 us

profile of v8, /device:TPU:0, one launch (start us, length us, event | category | flops | bytes accessed | tf_op | source)
XLA Modules:
  0.0 51.3 jit_solution(7888734312952910090)
XLA Ops:
  0.6 49.8 %shard_map.94 = (bf16[1024,128]{1,0:T(8,128)(2,1)S(1)}, bf16[1024,128]{1,0:T(8,128)(2,1)S(1)}, f32[512,128]{1,0:T(8,128)S(1)}) custom-call(bf16[1024,128]{1,0:T(8,128)(2,1)} %x.1, bf16[512,128]{1,0:T(8,128)(2,1)} %w_in.1, bf16[1,5,8,128,128]{4,3,2,1,0:T(8,128)(2,1)} %tv_in.1, s32[5,1,8]{2,1,0:T(1,128)} %bitcast.2, s32[5,1,8]{2,1,0:T(1,128)} %bitcast.3, ...), custom_call_target="tpu_custom_call" | custom-call | tf_op jit(solution)/shard_map/pallas_call | solution.py:676
  50.4 0.9 %shard_map.95 = (bf16[1024,128]{1,0:T(8,128)(2,1)}, bf16[1024,128]{1,0:T(8,128)(2,1)}, f32[512,128]{1,0:T(8,128)}) custom-call(bf16[1024,128]{1,0:T(8,128)(2,1)S(1)} %get-tuple-element.6.refs_0_, bf16[1024,128]{1,0:T(8,128)(2,1)S(1)} %get-tuple-element.7.refs_1_, f32[512,128]{1,0:T(8,128)S(1)} %get-tuple-element.8.refs_2_), custom_call_target="tpu_custom_call" | custom-call | tf_op jit(solution)/shard_map/pallas_call | solution.py:719
